TPU v7x, 32 devices: a whole 2x2x4 slice. The times are simulated.
32 devices in a mesh: dp: 2 (over x), seq: 16 (over z, y, core).
Axes of the slice: x: 2, y: 2, z: 4, core: 2. Of those that a mesh axis runs over, the one named last changes fastest.
Arguments:
- hidden: bfloat16 [2, 2048, 1024], P('dp', 'seq'), may hold values from -6 to 6
- letters: int32 [2, 2048], P('dp', 'seq'), may hold values from 0 to 3
- gate_input: bfloat16 [2, 2048, 1024], P('dp', 'seq'), may hold values from -6 to 6
- cotangent: bfloat16 [2, 2048, 1024], P('dp', 'seq'), may hold values from -6 to 6
- embedding: float32 [4, 1024], replicated, may hold values from -6 to 6
- filter_taps: bfloat16 [4, 128, 1024], P(None, 'seq'), may hold values from -0.25 to 0.25
Outputs:
- output: bfloat16 [2, 2048, 1024], P('dp', 'seq')
- hidden_grad: bfloat16 [2, 2048, 1024], P('dp', 'seq')
- gate_grad: bfloat16 [2, 2048, 1024], P('dp', 'seq')
- filter_grad: float32 [4, 128, 1024], P(None, 'seq')
- embedding_grad: float32 [4, 1024], replicated
All inputs are finite; a program needn't handle non-finite values.
Results may differ from a plain program's by a relative error of at most 0.0049.
Values may be sent and summed in bfloat16 or wider, within the bound.
No kernel may reach another device: no remote copies, remote signals or barrier semaphores. Data moves between devices by JAX's collectives and lax.ppermute only.
A program may use at most 128 MiB of HBM per device.

v0:
```python
import math

import jax
import jax.numpy as jnp
import numpy as np
from jax import lax
from jax.experimental import pallas as pl
from jax.experimental.pallas import tpu as pltpu
from jax.sharding import PartitionSpec as P

BLOCK = 512
COLS = 256
LANES = 128
STEP = 16

F32 = jnp.float32
BF16 = jnp.bfloat16


def tables():
    frequency = np.arange(BLOCK)[:, None]
    moment = np.arange(BLOCK)[None, :]
    angles = (frequency * moment % (2 * BLOCK)) * (2.0 * np.pi / (2 * BLOCK))
    sines = -np.sin(angles)
    sines[0] = 1.0 - 2.0 * (np.arange(BLOCK) % 2)
    forward = np.concatenate([np.cos(angles), sines], axis=0)
    weights = np.full((2 * BLOCK, 1), 1.0 / BLOCK)
    weights[0] = weights[BLOCK] = 0.5 / BLOCK
    backward = (forward * weights).T

    def halves(table):
        high = table.astype(jnp.bfloat16)
        return high, (table - high.astype(np.float64)).astype(jnp.bfloat16)

    return (*halves(forward), *halves(backward))


def iota(shape, axis):
    return lax.broadcasted_iota(jnp.int32, shape, axis)


def matmul(left, right):
    return jnp.dot(left, right, preferred_element_type=F32)


def swap_matrix():
    row, lane = iota((512, 512), 0), iota((1, 512), 1)
    source = ((lane >> 5) & 3) * 128 + (lane >> 7) * 32 + (lane & 31)
    return jnp.where(row == source, 1.0, 0.0).astype(BF16)


def channel_source(lane):
    group, spot = lane >> 5, lane & 31
    return jnp.where(spot < 16, 16 * group + spot, 271 - 16 * group - spot)


def gather_channels():
    row, lane = iota((256, 256), 0), iota((1, 256), 1)
    return jnp.where(row == channel_source(lane), 1.0, 0.0).astype(BF16)


def return_channels():
    row, lane = iota((256, 1), 0), iota((256, 256), 1)
    return jnp.where(channel_source(row) == lane, 1.0, 0.0).astype(BF16)


def pack_kernel(hidden_ref, letters_ref, gate_ref, upstream_ref, embedding_ref, taps_ref, send_ref):
    letters = letters_ref[...]
    square = iota((128, 128), 0) == iota((128, 128), 1)
    letter = jnp.sum(jnp.where(square, letters.astype(F32), 0.0), axis=1, keepdims=True)
    added = embedding_ref[0:1, :]
    for index in range(1, 4):
        added = jnp.where(letter == float(index), embedding_ref[index : index + 1, :], added)
    values = (hidden_ref[0].astype(F32) + added).astype(BF16)
    field_grad = (upstream_ref[0].astype(F32) * gate_ref[0].astype(F32)).astype(BF16)
    taps = taps_ref[pl.ds(2 * lax.axis_index("dp"), 2)].astype(F32).reshape(16, 1024).astype(BF16)
    gather = gather_channels()
    swap = swap_matrix()
    rows = []
    for part in (values, field_grad, taps):
        for u in range(4):
            pair = jnp.concatenate(
                [part[:, 128 * u : 128 * u + 128], part[:, 896 - 128 * u : 1024 - 128 * u]], axis=1
            )
            rows.append(matmul(pair, gather).astype(BF16))
    stacked = []
    for part in range(2):
        for m in range(8):
            block = rows[4 * part + m // 2][:, 128 * (m % 2) : 128 * (m % 2) + 128]
            stacked.append(jnp.concatenate([block[32 * q : 32 * q + 32] for q in range(4)], axis=1))
    moved = matmul(jnp.concatenate(stacked, axis=0), swap).astype(BF16)
    for part in range(2):
        for m in range(8):
            for d in range(4):
                start = 256 * part + 32 * m
                send_ref[4 * m + d, 32 * part : 32 * part + 32, :] = moved[
                    start : start + 32, 128 * d : 128 * d + 128
                ]
    stacked = []
    for m in range(8):
        block = rows[8 + m // 2][:, 128 * (m % 2) : 128 * (m % 2) + 128].astype(F32)
        stacked.append(jnp.concatenate([block[0:8], block[8:16]], axis=1))
    row, lane = iota((256, 512), 0), iota((1, 512), 1)
    spot = lane & 127
    source = jnp.where(spot < 64, (spot >> 5) * 128 + (lane >> 7) * 32 + (spot & 31), -1)
    spread = jnp.where(row == source, 1.0, 0.0).astype(BF16)
    moved = matmul(jnp.concatenate(stacked, axis=0).astype(BF16), spread)
    line = jnp.broadcast_to(letters.astype(F32), (8, 128))
    which, lane = iota((8, 128), 0), iota((8, 128), 1)
    shown = jnp.where(which == 0, pltpu.roll(line, 64, 1), jnp.where(which == 1, line, 0.0))
    shown = jnp.where(lane >= 64, shown, 0.0)
    for m in range(8):
        for d in range(4):
            piece = moved[8 * m : 8 * m + 8, 128 * d : 128 * d + 128] + shown
            send_ref[4 * m + d, 64:72, :] = piece.astype(BF16)


def spectra_step(spectra_ref, high_ref, low_ref, narrow, width, base, first):
    top, under = pl.ds(base, STEP), pl.ds(BLOCK + base, STEP)

    def load(start, size):
        return spectra_ref[top, start : start + size], spectra_ref[under, start : start + size]

    def twice(pair):
        return tuple(jnp.concatenate([part, part], axis=1) for part in pair)

    values, grads = load(0, COLS), load(COLS, COLS)
    own, mirror = twice(load(2 * COLS, LANES)), twice(load(2 * COLS + LANES, LANES))
    lane = iota((STEP, COLS), 1)
    sign = (1 - 2 * (iota((STEP, COLS), 0) & 1)).astype(F32)
    before_sign = jnp.where(lane >= width, sign, 0.0)
    after_sign = jnp.where(lane < COLS - width, sign, 0.0)
    real_row = iota((STEP, COLS), 0) == 0

    def with_earlier(pair):
        return tuple(part + before_sign * pltpu.roll(part, width, 1) for part in pair)

    def with_later(pair):
        return tuple(part + after_sign * pltpu.roll(part, COLS - width, 1) for part in pair)

    def settle(a, b, real, imaginary):
        if first:
            real = jnp.where(real_row, a[0] * b[0], real)
            imaginary = jnp.where(real_row, a[1] * b[1], imaginary)
        return real, imaginary

    def times(a, b):
        return settle(a, b, a[0] * b[0] - a[1] * b[1], a[0] * b[1] + a[1] * b[0])

    def times_conjugate(a, b):
        return settle(a, b, a[0] * b[0] + a[1] * b[1], a[1] * b[0] - a[0] * b[1])

    def plus(a, b):
        return a[0] + b[0], a[1] + b[1]

    def column_sum(pair):
        total = tuple(part[:, :LANES] + part[:, LANES:] for part in pair)
        shift = LANES // 2
        while shift >= narrow:
            total = tuple(part + pltpu.roll(part, shift, 1) for part in total)
            shift //= 2
        return total

    values_back, values_on = with_earlier(values), with_later(values)
    grads_back, grads_on = with_earlier(grads), with_later(grads)
    field = plus(times(values_back, own), times_conjugate(values_on, mirror))
    back = plus(times(grads_back, mirror), times_conjugate(grads_on, own))
    causal = column_sum(times_conjugate(grads, values_back))
    ahead = column_sum(times_conjugate(values_on, grads))
    lags = plus(causal, tuple(pltpu.roll(part, narrow // 2, 1) for part in ahead))
    for rows, part in ((top, 0), (under, 1)):
        for start, size, pair in ((0, COLS, field), (COLS, COLS, back), (2 * COLS, LANES, lags)):
            high = pair[part].astype(BF16)
            high_ref[rows, start : start + size] = high
            low_ref[rows, start : start + size] = (pair[part] - high.astype(F32)).astype(BF16)


def transforms(samples_ref, table_refs, spectra_ref, high_ref, low_ref, result_ref, narrow, width):
    forward_high, forward_low, backward_high, backward_low = table_refs
    for part in range(4):
        rows = slice(256 * part, 256 * part + 256)
        spectra_ref[rows, :] = matmul(forward_high[rows, :], samples_ref[...]) + matmul(
            forward_low[rows, :], samples_ref[...]
        )
    step = lambda base, first: spectra_step(
        spectra_ref, high_ref, low_ref, narrow, width, base, first
    )
    step(0, True)

    def body(index, carry):
        step(pl.multiple_of(index * STEP, STEP), False)
        return carry

    lax.fori_loop(1, BLOCK // STEP, body, 0)
    for part in range(2):
        rows = slice(256 * part, 256 * part + 256)
        result_ref[rows, :] = (
            matmul(backward_high[rows, :], high_ref[...])
            + matmul(backward_low[rows, :], high_ref[...])
            + matmul(backward_high[rows, :], low_ref[...])
        )


def letter_sums(values_grad, choice, belongs, narrow):
    high = values_grad.astype(BF16)
    low = (values_grad - high.astype(F32)).astype(BF16)
    sums = jnp.where(belongs, matmul(choice, high) + matmul(choice, low), 0.0)
    groups = sums.shape[0] // 4
    rows = [jnp.sum(sums[groups * a : groups * a + groups], axis=0, keepdims=True) for a in range(4)]
    total = jnp.concatenate(rows, axis=0)
    total = total[:, :LANES] + total[:, LANES:]
    shift = LANES // 2
    while shift >= narrow:
        total = total + pltpu.roll(total, shift, 1)
        shift //= 2
    return total


WORK = [
    pltpu.VMEM((BLOCK, 3 * COLS), BF16),
    pltpu.VMEM((2 * BLOCK, 3 * COLS), F32),
    pltpu.VMEM((2 * BLOCK, 2 * COLS + LANES), BF16),
    pltpu.VMEM((2 * BLOCK, 2 * COLS + LANES), BF16),
    pltpu.VMEM((BLOCK, 2 * COLS + LANES), F32),
]


def middle_kernel(
    norming, receive_ref, fh_ref, fl_ref, bh_ref, bl_ref, send_ref,
    samples_ref, spectra_ref, high_ref, low_ref, result_ref,
):
    swap = swap_matrix()
    places = [(part, u, s) for part in range(2) for u in range(2) for s in range(4)]
    stacked = []
    for part, u, s in places:
        pieces = [
            receive_ref[16 * d + 4 * (2 * u + j) + s, 32 * part : 32 * part + 32, :]
            for j in range(2)
            for d in range(2)
        ]
        stacked.append(jnp.concatenate(pieces, axis=1))
    moved = matmul(jnp.concatenate(stacked, axis=0), swap).astype(BF16)
    for index, (part, u, s) in enumerate(places):
        for q in range(4):
            start = 128 * s + 32 * q
            samples_ref[start : start + 32, 256 * part + 128 * u : 256 * part + 128 * u + 128] = moved[
                32 * index : 32 * index + 32, 128 * q : 128 * q + 128
            ]
    tails = receive_ref[:, 64:72, :].astype(F32)
    row, lane = iota((128, 256), 0), iota((1, 256), 1)
    spot = (lane & 31) ^ ((lane >> 7) << 4)
    for d in range(2):
        tail = tails[16 * d : 16 * d + 16].reshape(128, 128).astype(BF16)
        for k in range(2):
            spread = jnp.where(row == 32 * k + spot, 1.0, 0.0).astype(BF16)
            start = 128 * (2 * d + k)
            samples_ref[start : start + 128, 512:768] = matmul(tail, spread).astype(BF16)
    transforms(
        samples_ref, (fh_ref, fl_ref, bh_ref, bl_ref), spectra_ref, high_ref, low_ref, result_ref, 32, 64
    )
    field_pieces = []
    for part, u, s in places:
        pieces = [
            result_ref[128 * s + 32 * q : 128 * s + 32 * q + 32, 256 * part + 128 * u : 256 * part + 128 * u + 128]
            for q in range(4)
        ]
        field_pieces.append(jnp.concatenate(pieces, axis=1).astype(BF16))
    moved = matmul(jnp.concatenate(field_pieces, axis=0), swap).astype(BF16)
    for index, (part, u, s) in enumerate(places):
        for j in range(2):
            for d in range(2):
                group = 2 * j + d
                send_ref[16 * d + 4 * (2 * u + j) + s, 32 * part : 32 * part + 32, :] = moved[
                    32 * index : 32 * index + 32, 128 * group : 128 * group + 128
                ]
    quarter = iota((128, 128), 1) >> 5
    lags = result_ref[0:128, 512:640]
    for k in range(1, 4):
        lags = jnp.where(quarter == k, result_ref[128 * k : 128 * k + 128, 512:640], lags)
    lags = (lags * norming).reshape(16, 8, 128).astype(BF16)
    send_ref[0:16, 64:72, :] = lags
    send_ref[16:32, 64:72, :] = lags
    line = iota((32, 128), 1)
    letters = jnp.where(line < 64, pltpu.roll(tails[:, 0, :], 64, 1), tails[:, 1, :])
    source = iota((32, 128), 0)
    choice = []
    for a in range(4):
        chosen = jnp.where(letters == float(a), 1.0, 0.0)
        choice.append(
            jnp.concatenate([jnp.where((source & 3) == s, chosen, 0.0) for s in range(4)], axis=1)
        )
    choice = jnp.concatenate(choice, axis=0).astype(BF16)
    source = iota((128, 256), 0) & 31
    belongs = (((source >> 2) & 3) * 2 + (source >> 4)) == (iota((128, 256), 1) >> 5)
    sums = letter_sums(result_ref[:, 256:512], choice, belongs, 32) * norming
    high = sums.astype(BF16).astype(F32)
    tile = jnp.concatenate([high, sums - high], axis=0).astype(BF16)
    for index in range(32):
        send_ref[index, 72:80, :] = tile


def finish_kernel(receive_ref, gate_ref, upstream_ref, out_ref, hidden_ref, gated_ref, filter_ref, embedding_ref):
    swap = swap_matrix()
    back = return_channels()
    stacked = []
    for part in range(2):
        for m in range(8):
            pieces = [receive_ref[4 * m + d, 32 * part : 32 * part + 32, :] for d in range(4)]
            stacked.append(jnp.concatenate(pieces, axis=1))
    moved = matmul(jnp.concatenate(stacked, axis=0), swap).astype(BF16)
    for u in range(4):
        halves = []
        for part in range(2):
            columns = []
            for m in (2 * u, 2 * u + 1):
                start = 256 * part + 32 * m
                columns.append(
                    jnp.concatenate(
                        [moved[start : start + 32, 128 * q : 128 * q + 128] for q in range(4)], axis=0
                    )
                )
            halves.append(matmul(jnp.concatenate(columns, axis=1), back))
        for start, lane in ((128 * u, 0), (896 - 128 * u, 128)):
            there = slice(start, start + 128)
            field = halves[0][:, lane : lane + 128]
            out_ref[0, :, there] = (gate_ref[0, :, there].astype(F32) * field).astype(BF16)
            gated_ref[0, :, there] = (upstream_ref[0, :, there].astype(F32) * field).astype(BF16)
            hidden_ref[0, :, there] = halves[1][:, lane : lane + 128].astype(BF16)
    tails = receive_ref[:, 64:80, :].astype(F32)
    stacked = [
        jnp.concatenate([tails[4 * m + d, 0:8, :] for d in range(4)], axis=1) for m in range(8)
    ]
    moved = matmul(jnp.concatenate(stacked, axis=0).astype(BF16), swap)
    quarter = iota((8, 128), 1) >> 5
    for u in range(4):
        columns = []
        for m in (2 * u, 2 * u + 1):
            rows = [moved[8 * m : 8 * m + 8, 128 * k : 128 * k + 128] for k in range(4)]
            sums = tails[4 * m, 8:16, :]
            for d in range(1, 4):
                sums = jnp.where(quarter == d, tails[4 * m + d, 8:16, :], sums)
            columns.append(jnp.concatenate(rows + [sums], axis=0))
        done = matmul(jnp.concatenate(columns, axis=1).astype(BF16), back)
        for start, lane in ((128 * u, 0), (896 - 128 * u, 128)):
            there = slice(start, start + 128)
            filter_ref[:, :, there] = done[0:32, lane : lane + 128].reshape(4, 8, 128)
            embedding_ref[:, there] = done[32:36, lane : lane + 128] + done[36:40, lane : lane + 128]


def call(kernel, shapes, scratch=()):
    return pl.pallas_call(
        kernel,
        out_shape=shapes,
        scratch_shapes=scratch,
        compiler_params=pltpu.CompilerParams(vmem_limit_bytes=48 * 1024 * 1024),
    )


def packed_device(hidden, letters, gate_input, cotangent, embedding, filter_taps, norming):
    send = call(pack_kernel, jax.ShapeDtypeStruct((32, 72, 128), BF16))(
        hidden, letters, gate_input, cotangent, embedding, filter_taps
    )
    received = lax.all_to_all(send, ("dp", "seq"), 0, 0, tiled=True)

    def middle(*refs):
        middle_kernel(norming, *refs)

    send = call(middle, jax.ShapeDtypeStruct((32, 80, 128), BF16), WORK)(received, *tables())
    received = lax.all_to_all(send, ("dp", "seq"), 0, 0, tiled=True)
    shape = jax.ShapeDtypeStruct(hidden.shape, BF16)
    output, hidden_grad, gate_grad, filter_grad, embedding_grad = call(
        finish_kernel,
        (
            shape,
            shape,
            shape,
            jax.ShapeDtypeStruct(filter_taps.shape, F32),
            jax.ShapeDtypeStruct(embedding.shape, F32),
        ),
    )(received, gate_input, cotangent)
    return output, hidden_grad, gate_grad, filter_grad, embedding_grad


def plain_kernel(
    narrow, width, samples_ref, letters_ref, fh_ref, fl_ref, bh_ref, bl_ref,
    field_ref, back_ref, lags_ref, sums_ref, spectra_ref, high_ref, low_ref, result_ref,
):
    transforms(
        samples_ref, (fh_ref, fl_ref, bh_ref, bl_ref), spectra_ref, high_ref, low_ref, result_ref, narrow, width
    )
    field_ref[...] = result_ref[:, 0:256].astype(BF16)
    back_ref[...] = result_ref[:, 256:512].astype(BF16)
    lags_ref[...] = result_ref[:, 512:640]
    letters = letters_ref[...]
    groups = COLS // narrow
    choice = jnp.concatenate(
        [jnp.where(letters == float(a), 1.0, 0.0) for a in range(4)], axis=0
    ).astype(BF16)
    shape = (4 * groups, COLS)
    belongs = (iota(shape, 0) & (groups - 1)) == iota(shape, 1) // narrow
    sums_ref[...] = letter_sums(result_ref[:, 256:512], choice, belongs, narrow)


def plain_device(hidden, letters, gate_input, cotangent, embedding, filter_taps, norming):
    axes = ("dp", "seq")
    copies, stretches = lax.axis_size("dp"), lax.axis_size("seq")
    devices = copies * stretches
    stretch, channels = hidden.shape[1], hidden.shape[2]
    narrow = channels // devices
    half = narrow // 2
    blocks = stretch * stretches // BLOCK
    low = np.arange(channels // 2).reshape(devices, half)
    order = np.concatenate([low, channels - 1 - low], axis=1).reshape(-1)
    restore = np.argsort(order)
    onehot = (letters[0][:, None] == jnp.arange(embedding.shape[0], dtype=jnp.int32)[None, :]).astype(F32)
    added = jnp.dot(onehot, embedding, precision=lax.Precision.HIGHEST)
    values = (hidden[0].astype(F32) + added).astype(BF16)
    gate_wide, upstream = gate_input[0].astype(F32), cotangent[0].astype(F32)
    field_grad = (upstream * gate_wide).astype(BF16)

    def scatter(array):
        parts = jnp.take(array, order, axis=1).reshape(stretch, devices, narrow).swapaxes(0, 1)
        parts = lax.all_to_all(parts, axes, 0, 0, tiled=True)
        parts = parts.reshape(copies, blocks, BLOCK, narrow)
        return parts.transpose(2, 1, 0, 3).reshape(BLOCK, COLS)

    def gather(columns):
        parts = columns.reshape(BLOCK, blocks, copies, narrow).transpose(2, 1, 0, 3)
        parts = parts.reshape(devices, stretch, narrow)
        parts = lax.all_to_all(parts, axes, 0, 0, tiled=True)
        return jnp.take(parts.swapaxes(0, 1).reshape(stretch, channels), restore, axis=1)

    taps = lax.all_gather(filter_taps, "seq", axis=1, tiled=True).reshape(BLOCK, channels)
    mine = lax.axis_index("dp") * stretches + lax.axis_index("seq")
    own = lax.dynamic_slice_in_dim(jnp.take(taps, order, axis=1), mine * narrow, narrow, axis=1)
    mirror = jnp.roll(own, half, axis=1)
    repeats = LANES // narrow
    samples = jnp.concatenate(
        [scatter(values), scatter(field_grad), jnp.tile(own, (1, repeats)), jnp.tile(mirror, (1, repeats))], axis=1
    )
    marks = lax.all_gather(letters[0].astype(F32), axes, tiled=True)
    marks = marks.reshape(copies, blocks, BLOCK).swapaxes(0, 1).reshape(copies * blocks, BLOCK)

    def kernel(*refs):
        plain_kernel(narrow, copies * narrow, *refs)

    field, back, lags, sums = call(
        kernel,
        (
            jax.ShapeDtypeStruct((BLOCK, COLS), BF16),
            jax.ShapeDtypeStruct((BLOCK, COLS), BF16),
            jax.ShapeDtypeStruct((BLOCK, LANES), F32),
            jax.ShapeDtypeStruct((embedding.shape[0], LANES), F32),
        ),
        WORK[1:],
    )(samples, marks, *tables())
    small = jnp.concatenate([lags[:, :narrow], sums[:, :narrow]], axis=0) * norming
    small = jnp.take(lax.all_gather(small, axes, axis=1, tiled=True), restore, axis=1)
    rows = filter_taps.shape[1]
    filter_grad = lax.dynamic_slice_in_dim(
        small[:BLOCK].reshape(filter_taps.shape[0], stretch, channels), lax.axis_index("seq") * rows, rows, axis=1
    )
    field_rows, grad_rows = gather(field).astype(F32), gather(back)
    output = (gate_wide * field_rows).astype(BF16)[None]
    gate_grad = (upstream * field_rows).astype(BF16)[None]
    return output, grad_rows[None], gate_grad, filter_grad, small[BLOCK:]


def per_device(hidden, letters, gate_input, cotangent, embedding, filter_taps):
    copies, stretches = lax.axis_size("dp"), lax.axis_size("seq")
    norming = 1.0 / math.sqrt(copies * hidden.shape[0] * hidden.shape[1] * stretches)
    device = packed_device if (copies, stretches) == (2, 16) else plain_device
    return device(hidden, letters, gate_input, cotangent, embedding, filter_taps, norming)


def solution(mesh):
    return jax.shard_map(
        per_device,
        mesh=mesh,
        in_specs=(
            P("dp", "seq", None),
            P("dp", "seq"),
            P("dp", "seq", None),
            P("dp", "seq", None),
            P(),
            P(None, "seq", None),
        ),
        out_specs=(
            P("dp", "seq", None),
            P("dp", "seq", None),
            P("dp", "seq", None),
            P(None, "seq", None),
            P(),
        ),
        check_vma=False,
    )
```

profile of v0, /device:TPU:0, one launch (start us, length us, event | category | flops | bytes accessed | tf_op | source)
XLA Modules:
  0.0 70.8 jit_solution(13205820638261467948)
XLA Ops:
  0.6 0.0 copy-start
  0.6 0.0 copy-start.1
  0.7 0.0 copy-start.4
  0.7 1.1 %copy-done.4 = bf16[1,128,1024]{2,1,0:T(8,128)(2,1)S(1)} copy-done((bf16[1,128,1024]{2,1,0:T(8,128)(2,1)S(1)}, bf16[1,128,1024]{2,1,0:T(8,128)(2,1)}, u32[]{:S(2)}) %copy-start.4) | copy-done | bytes 262168
  1.8 0.0 copy-start.6
  1.8 0.9 %copy-done.6 = bf16[1,128,1024]{2,1,0:T(8,128)(2,1)S(1)} copy-done((bf16[1,128,1024]{2,1,0:T(8,128)(2,1)S(1)}, bf16[1,128,1024]{2,1,0:T(8,128)(2,1)}, u32[]{:S(2)}) %copy-start.6) | copy-done | bytes 262168
  2.7 0.0 copy-start.8
  2.7 0.9 %copy-done.8 = bf16[1,128,1024]{2,1,0:T(8,128)(2,1)S(1)} copy-done((bf16[1,128,1024]{2,1,0:T(8,128)(2,1)S(1)}, bf16[1,128,1024]{2,1,0:T(8,128)(2,1)}, u32[]{:S(2)}) %copy-start.8) | copy-done | bytes 262168
  3.7 0.8 %copy-done.9 = bf16[4,8,1024]{2,1,0:T(8,128)(2,1)S(1)} copy-done((bf16[4,8,1024]{2,1,0:T(8,128)(2,1)S(1)}, bf16[4,8,1024]{2,1,0:T(8,128)(2,1)}, u32[]{:S(2)}) %copy-start.9) | copy-done | bytes 65560
  4.5 0.7 %copy-done.10 = f32[4,1024]{1,0:T(4,128)S(1)} copy-done((f32[4,1024]{1,0:T(4,128)S(1)}, f32[4,1024]{1,0:T(4,128)}, u32[]{:S(2)}) %copy-start.10) | copy-done | bytes 16408
  5.2 0.7 copy-done.11
  5.9 0.8 %shard_map.137 = bf16[32,72,128]{2,1,0:T(8,128)(2,1)S(1)} custom-call(bf16[1,128,1024]{2,1,0:T(8,128)(2,1)S(1)} %copy-done.8, s32[1,128]{1,0:T(1,128)S(1)} %copy-done.11, bf16[1,128,1024]{2,1,0:T(8,128)(2,1)S(1)} %copy-done.4, bf16[1,128,1024]{2,1,0:T(8,128)(2,1)S(1)} %copy-done.6, f32[4,1024]{1,0:T(4,128)S(1)} %copy-done.10, bf16[4,8,1024]{2,1,0:T(8,128)(2,1)S(1)} %copy-done.9), custom_call_target="tpu_custom_call" | custom-call | tf_op jit(solution)/shard_map/pallas_call | solution.py:360
  6.7 24.4 %all_to_all.10.refs_0_ = bf16[32,72,128]{2,1,0:T(8,128)(2,1)S(1)} all-to-all(bf16[32,72,128]{2,1,0:T(8,128)(2,1)S(1)} %shard_map.137), channel_id=1, replica_groups=mesh['dp'=2,'seq'=16] {'dp','seq'}, dimensions={0} | all-to-all | bytes 1179648 | tf_op jit(solution)/shard_map/all_to_all | solution.py:363
  31.1 0.0 copy-done
  31.1 0.0 copy-done.1
  31.1 1.2 %copy-done.2 = bf16[1024,512]{1,0:T(8,128)(2,1)S(1)} copy-done((bf16[1024,512]{1,0:T(8,128)(2,1)S(1)}, bf16[1024,512]{1,0:T(8,128)(2,1)}, u32[]{:S(2)}) %copy-start.2) | copy-done | bytes 1048600
  32.3 1.2 %copy-done.3 = bf16[1024,512]{1,0:T(8,128)(2,1)S(1)} copy-done((bf16[1024,512]{1,0:T(8,128)(2,1)S(1)}, bf16[1024,512]{1,0:T(8,128)(2,1)}, u32[]{:S(2)}) %copy-start.3) | copy-done | bytes 1048600
  33.5 14.9 %shard_map.138 = bf16[32,80,128]{2,1,0:T(8,128)(2,1)S(1)} custom-call(bf16[32,72,128]{2,1,0:T(8,128)(2,1)S(1)} %all_to_all.10.refs_0_, bf16[1024,512]{1,0:T(8,128)(2,1)S(1)} %copy-done.3, bf16[1024,512]{1,0:T(8,128)(2,1)S(1)} %copy-done.2, bf16[512,1024]{1,0:T(8,128)(2,1)S(1)} %copy-done.1, bf16[512,1024]{1,0:T(8,128)(2,1)S(1)} %copy-done), custom_call_target="tpu_custom_call" | custom-call | tf_op jit(solution)/shard_map/pallas_call | solution.py:368
  48.4 0.0 copy-start.5
  48.4 0.0 copy-start.7
  48.4 20.8 %all_to_all.11.receive_ref = bf16[32,80,128]{2,1,0:T(8,128)(2,1)S(1)} all-to-all(bf16[32,80,128]{2,1,0:T(8,128)(2,1)S(1)} %shard_map.138), channel_id=1, replica_groups=mesh['dp'=2,'seq'=16] {'dp','seq'}, dimensions={0} | all-to-all | bytes 1310720 | tf_op jit(solution)/shard_map/all_to_all | solution.py:369
  69.2 0.0 copy-done.5
  69.2 0.0 copy-done.7
  69.2 1.6 %shard_map.139 = (bf16[1,128,1024]{2,1,0:T(8,128)(2,1)}, bf16[1,128,1024]{2,1,0:T(8,128)(2,1)}, bf16[1,128,1024]{2,1,0:T(8,128)(2,1)}, f32[4,8,1024]{2,1,0:T(8,128)}, f32[4,1024]{1,0:T(4,128)}) custom-call(bf16[32,80,128]{2,1,0:T(8,128)(2,1)S(1)} %all_to_all.11.receive_ref, bf16[1,128,1024]{2,1,0:T(8,128)(2,1)S(1)} %copy-done.5, ...), custom_call_target="tpu_custom_call" | custom-call | tf_op jit(solution)/shard_map/pallas_call | solution.py:371
  (5 shorter events, 0.0 us)
Async XLA Ops:
  0.6 30.5 %copy-start = (bf16[512,1024]{1,0:T(8,128)(2,1)S(1)}, bf16[512,1024]{1,0:T(8,128)(2,1)}, u32[]{:S(2)}) copy-start(bf16[512,1024]{1,0:T(8,128)(2,1)} %constant.11.clone.refs_4_) | copy-start | bytes 3145732
  0.6 30.4 %copy-start.1 = (bf16[512,1024]{1,0:T(8,128)(2,1)S(1)}, bf16[512,1024]{1,0:T(8,128)(2,1)}, u32[]{:S(2)}) copy-start(bf16[512,1024]{1,0:T(8,128)(2,1)} %constant.10.clone.refs_3_) | copy-start | bytes 3145732
  0.7 1.1 %copy-start.4 = (bf16[1,128,1024]{2,1,0:T(8,128)(2,1)S(1)}, bf16[1,128,1024]{2,1,0:T(8,128)(2,1)}, u32[]{:S(2)}) copy-start(bf16[1,128,1024]{2,1,0:T(8,128)(2,1)} %gate_ref.3) | copy-start | bytes 786436
  1.8 0.9 %copy-start.6 = (bf16[1,128,1024]{2,1,0:T(8,128)(2,1)S(1)}, bf16[1,128,1024]{2,1,0:T(8,128)(2,1)}, u32[]{:S(2)}) copy-start(bf16[1,128,1024]{2,1,0:T(8,128)(2,1)} %upstream_ref.3) | copy-start | bytes 786436
  2.7 0.9 %copy-start.8 = (bf16[1,128,1024]{2,1,0:T(8,128)(2,1)S(1)}, bf16[1,128,1024]{2,1,0:T(8,128)(2,1)}, u32[]{:S(2)}) copy-start(bf16[1,128,1024]{2,1,0:T(8,128)(2,1)} %hidden_ref.1) | copy-start | bytes 786436
  3.7 0.8 %copy-start.9 = (bf16[4,8,1024]{2,1,0:T(8,128)(2,1)S(1)}, bf16[4,8,1024]{2,1,0:T(8,128)(2,1)}, u32[]{:S(2)}) copy-start(bf16[4,8,1024]{2,1,0:T(8,128)(2,1)} %taps_ref.1) | copy-start | bytes 196612
  4.5 0.7 %copy-start.10 = (f32[4,1024]{1,0:T(4,128)S(1)}, f32[4,1024]{1,0:T(4,128)}, u32[]{:S(2)}) copy-start(f32[4,1024]{1,0:T(4,128)} %embedding_ref.1) | copy-start | bytes 49156
  5.2 0.7 copy-start.11
  31.1 1.2 %copy-start.2 = (bf16[1024,512]{1,0:T(8,128)(2,1)S(1)}, bf16[1024,512]{1,0:T(8,128)(2,1)}, u32[]{:S(2)}) copy-start(bf16[1024,512]{1,0:T(8,128)(2,1)} %constant.9.clone.refs_2_) | copy-start | bytes 3145732
  32.3 1.2 %copy-start.3 = (bf16[1024,512]{1,0:T(8,128)(2,1)S(1)}, bf16[1024,512]{1,0:T(8,128)(2,1)}, u32[]{:S(2)}) copy-start(bf16[1024,512]{1,0:T(8,128)(2,1)} %constant.8.clone.refs_1_) | copy-start | bytes 3145732
  48.4 20.8 %copy-start.5 = (bf16[1,128,1024]{2,1,0:T(8,128)(2,1)S(1)}, bf16[1,128,1024]{2,1,0:T(8,128)(2,1)}, u32[]{:S(2)}) copy-start(bf16[1,128,1024]{2,1,0:T(8,128)(2,1)} %gate_ref.3) | copy-start | bytes 786436
  48.4 20.8 %copy-start.7 = (bf16[1,128,1024]{2,1,0:T(8,128)(2,1)S(1)}, bf16[1,128,1024]{2,1,0:T(8,128)(2,1)}, u32[]{:S(2)}) copy-start(bf16[1,128,1024]{2,1,0:T(8,128)(2,1)} %upstream_ref.3) | copy-start | bytes 786436
where the time goes:
time: 71.2 us; the launch traced here: 70.8 us
  blocking collectives  45.2 us (63%)
  Pallas kernels  17.2 us (24%)
  local copies, waits for them, and re-layouts  7.68 us (11%)
    all_to_all x2, blocking collectives, packed_device(): received = lax.all_to_all(send, ('dp', 'seq'), 0, 0, tiled=True)  45.2 us
    pallas_call x1, Pallas kernels, packed_device(): call(middle, jax.ShapeDtypeStruct((32, 80, 128), BF16), WORK)  14.9 us
    unnamed x24, local copies, waits for them, and re-layouts  7.68 us
    pallas_call x1, Pallas kernels, packed_device(): call(finish_kernel, (shape, shape, shape, jax.ShapeDtypeStruct(filter_tap...  1.58 us

commit v1 on v0

v1 whole, which is shorter than its diff:
```python
import math

import jax
import jax.numpy as jnp
import numpy as np
from jax import lax
from jax.experimental import pallas as pl
from jax.experimental.pallas import tpu as pltpu
from jax.sharding import PartitionSpec as P

BLOCK = 512
COLS = 256
LANES = 128
STEP = 16
CHUNK = 128
GROUP = 2

F32 = jnp.float32
BF16 = jnp.bfloat16


def tables():
    frequency = np.arange(BLOCK)[:, None]
    moment = np.arange(BLOCK)[None, :]
    angles = (frequency * moment % (2 * BLOCK)) * (2.0 * np.pi / (2 * BLOCK))
    sines = -np.sin(angles)
    sines[0] = 1.0 - 2.0 * (np.arange(BLOCK) % 2)
    forward = np.stack([np.cos(angles).reshape(-1, CHUNK, BLOCK), sines.reshape(-1, CHUNK, BLOCK)], axis=1)
    forward = forward.reshape(2 * BLOCK, BLOCK)
    weights = np.full((2 * BLOCK, 1), 1.0 / BLOCK)
    weights[0] = weights[CHUNK] = 0.5 / BLOCK
    backward = (forward * weights).T

    def halves(table):
        high = table.astype(jnp.bfloat16)
        return high, (table - high.astype(np.float64)).astype(jnp.bfloat16)

    return (*halves(forward), *halves(backward))


def iota(shape, axis):
    return lax.broadcasted_iota(jnp.int32, shape, axis)


def matmul(left, right):
    return jnp.dot(left, right, preferred_element_type=F32)


def swap_matrix():
    row, lane = iota((512, 512), 0), iota((1, 512), 1)
    source = ((lane >> 5) & 3) * 128 + (lane >> 7) * 32 + (lane & 31)
    return jnp.where(row == source, 1.0, 0.0).astype(BF16)


def channel_source(lane):
    group, spot = lane >> 5, lane & 31
    return jnp.where(spot < 16, 16 * group + spot, 271 - 16 * group - spot)


def gather_channels():
    row, lane = iota((256, 256), 0), iota((1, 256), 1)
    return jnp.where(row == channel_source(lane), 1.0, 0.0).astype(BF16)


def return_channels():
    row, lane = iota((256, 1), 0), iota((256, 256), 1)
    return jnp.where(channel_source(row) == lane, 1.0, 0.0).astype(BF16)


def copy_in(pairs, sems):
    copies = [pltpu.make_async_copy(source, target, sems.at[index]) for index, (source, target) in enumerate(pairs)]
    for copy in copies:
        copy.start()
    return copies


def gathered_rows(part):
    gather = gather_channels()
    rows = []
    for u in range(4):
        pair = jnp.concatenate([part[:, 128 * u : 128 * u + 128], part[:, 896 - 128 * u : 1024 - 128 * u]], axis=1)
        rows.append(matmul(pair, gather).astype(BF16))
    return rows


def send_stretch(part, send_ref, place):
    rows = gathered_rows(part)
    stacked = []
    for m in range(8):
        block = rows[m // 2][:, 128 * (m % 2) : 128 * (m % 2) + 128]
        stacked.append(jnp.concatenate([block[32 * q : 32 * q + 32] for q in range(4)], axis=1))
    moved = matmul(jnp.concatenate(stacked, axis=0), swap_matrix()).astype(BF16)
    for m in range(8):
        for d in range(4):
            send_ref[4 * m + d, place : place + 32, :] = moved[32 * m : 32 * m + 32, 128 * d : 128 * d + 128]


def pack_kernel(
    hidden_hbm, letters_hbm, gate_hbm, upstream_hbm, embedding_hbm, taps_hbm, send_ref,
    hidden_ref, letters_ref, gate_ref, upstream_ref, embedding_ref, taps_ref, sems,
):
    copies = copy_in(
        [
            (letters_hbm, letters_ref),
            (embedding_hbm, embedding_ref),
            (taps_hbm.at[pl.ds(2 * lax.axis_index("dp"), 2)], taps_ref),
            (hidden_hbm, hidden_ref),
            (gate_hbm, gate_ref),
            (upstream_hbm, upstream_ref),
        ],
        sems,
    )
    for copy in copies[:3]:
        copy.wait()
    letters = letters_ref[...]
    rows = gathered_rows(taps_ref[...].astype(F32).reshape(16, 1024).astype(BF16))
    stacked = []
    for m in range(8):
        block = rows[m // 2][:, 128 * (m % 2) : 128 * (m % 2) + 128].astype(F32)
        stacked.append(jnp.concatenate([block[0:8], block[8:16]], axis=1))
    row, lane = iota((256, 512), 0), iota((1, 512), 1)
    spot = lane & 127
    source = jnp.where(spot < 64, (spot >> 5) * 128 + (lane >> 7) * 32 + (spot & 31), -1)
    spread = jnp.where(row == source, 1.0, 0.0).astype(BF16)
    moved = matmul(jnp.concatenate(stacked, axis=0).astype(BF16), spread)
    line = jnp.broadcast_to(letters.astype(F32), (8, 128))
    which, lane = iota((8, 128), 0), iota((8, 128), 1)
    shown = jnp.where(which == 0, pltpu.roll(line, 64, 1), jnp.where(which == 1, line, 0.0))
    shown = jnp.where(lane >= 64, shown, 0.0)
    for m in range(8):
        for d in range(4):
            piece = moved[8 * m : 8 * m + 8, 128 * d : 128 * d + 128] + shown
            send_ref[4 * m + d, 64:72, :] = piece.astype(BF16)
    square = iota((128, 128), 0) == iota((128, 128), 1)
    letter = jnp.sum(jnp.where(square, letters.astype(F32), 0.0), axis=1, keepdims=True)
    added = embedding_ref[0:1, :]
    for index in range(1, 4):
        added = jnp.where(letter == float(index), embedding_ref[index : index + 1, :], added)
    copies[3].wait()
    send_stretch((hidden_ref[0].astype(F32) + added).astype(BF16), send_ref, 0)
    copies[4].wait()
    copies[5].wait()
    send_stretch((upstream_ref[0].astype(F32) * gate_ref[0].astype(F32)).astype(BF16), send_ref, 32)


def load_pair(ref, base, start, size):
    return tuple(
        [ref[row : row + STEP, lane : lane + LANES] for lane in range(start, start + size, LANES)]
        for row in (base, base + CHUNK)
    )


def with_neighbours(pair, width):
    lane = iota((STEP, LANES), 1)
    sign = (1 - 2 * (iota((STEP, LANES), 0) & 1)).astype(F32)
    if width == LANES // 2:
        high_sign = jnp.where(lane >= width, sign, 0.0)
        low_sign = sign - high_sign
        back, on = [], []
        for first, second in pair:
            turned, other = pltpu.roll(first, width, 1), pltpu.roll(second, width, 1)
            between = sign * jnp.where(lane < width, turned, other)
            back.append([first + high_sign * turned, second + between])
            on.append([first + between, second + low_sign * other])
        return tuple(back), tuple(on)
    lane = iota((STEP, COLS), 1)
    sign = (1 - 2 * (iota((STEP, COLS), 0) & 1)).astype(F32)
    both = []
    for shift, keep in ((width, lane >= width), (COLS - width, lane < COLS - width)):
        signs = jnp.where(keep, sign, 0.0)
        moved = []
        for parts in pair:
            wide = jnp.concatenate(parts, axis=1)
            wide = wide + signs * pltpu.roll(wide, shift, 1)
            moved.append([wide[:, :LANES], wide[:, LANES:]])
        both.append(tuple(moved))
    return tuple(both)


def products(first):
    real_row = iota((STEP, LANES), 0) == 0

    def settle(a, b, real, imaginary):
        if first:
            real = jnp.where(real_row, a[0] * b[0], real)
            imaginary = jnp.where(real_row, a[1] * b[1], imaginary)
        return real, imaginary

    def times(a, b):
        return settle(a, b, a[0] * b[0] - a[1] * b[1], a[0] * b[1] + a[1] * b[0])

    def times_conjugate(a, b):
        return settle(a, b, a[0] * b[0] + a[1] * b[1], a[1] * b[0] - a[0] * b[1])

    return times, times_conjugate


def plus(a, b):
    return a[0] + b[0], a[1] + b[1]


def column(pair, index):
    return pair[0][index], pair[1][index]


def store_split(high_ref, low_ref, base, start, pair):
    for row, part in ((base, 0), (base + CHUNK, 1)):
        high = pair[part].astype(BF16)
        high_ref[row : row + STEP, start : start + LANES] = high
        low_ref[row : row + STEP, start : start + LANES] = (pair[part] - high.astype(F32)).astype(BF16)


def spectra_step(spectra_ref, high_ref, low_ref, narrow, width, base, first):
    times, times_conjugate = products(first)
    back, on = with_neighbours(load_pair(spectra_ref, base, 0, COLS), width)
    own = column(load_pair(spectra_ref, base, 2 * COLS, LANES), 0)
    mirror = column(load_pair(spectra_ref, base, 2 * COLS + LANES, LANES), 0)
    for index in range(2):
        field = plus(times(column(back, index), own), times_conjugate(column(on, index), mirror))
        store_split(high_ref, low_ref, base, LANES * index, field)
    grads = load_pair(spectra_ref, base, COLS, COLS)
    causal, ahead = None, None
    for index in range(2):
        one = times_conjugate(column(grads, index), column(back, index))
        two = times_conjugate(column(on, index), column(grads, index))
        causal = one if causal is None else plus(causal, one)
        ahead = two if ahead is None else plus(ahead, two)
    lags = plus(causal, tuple(pltpu.roll(part, narrow // 2, 1) for part in ahead))
    store_split(high_ref, low_ref, base, 2 * COLS, lags)
    back, on = with_neighbours(grads, width)
    for index in range(2):
        wanted = plus(times(column(back, index), mirror), times_conjugate(column(on, index), own))
        store_split(high_ref, low_ref, base, COLS + LANES * index, wanted)


def transforms(samples_ref, table_refs, copies, spectra_ref, high_ref, low_ref, result_ref, narrow, width):
    forward_high, forward_low, backward_high, backward_low = table_refs
    chunks = BLOCK // CHUNK

    def forward(chunk):
        rows = slice(2 * CHUNK * chunk, 2 * CHUNK * (chunk + 1))
        for columns in (slice(0, COLS), slice(2 * COLS, 3 * COLS), slice(COLS, 2 * COLS)):
            spectra_ref[rows, columns] = matmul(forward_high[rows, :], samples_ref[:, columns]) + matmul(
                forward_low[rows, :], samples_ref[:, columns]
            )

    forward(0)
    for chunk in range(chunks):
        if chunk + 1 < chunks:
            forward(chunk + 1)
        for base in range(2 * CHUNK * chunk, 2 * CHUNK * chunk + CHUNK, STEP):
            spectra_step(spectra_ref, high_ref, low_ref, narrow, width, base, base == 0)
        if chunk + 1 == GROUP:
            for copy in copies:
                copy.wait()
        if (chunk + 1) % GROUP == 0:
            span = slice(2 * CHUNK * (chunk + 1 - GROUP), 2 * CHUNK * (chunk + 1))
            for columns in (slice(0, COLS), slice(COLS, 2 * COLS), slice(2 * COLS, 2 * COLS + LANES)):
                made = (
                    matmul(backward_high[:, span], high_ref[span, columns])
                    + matmul(backward_low[:, span], high_ref[span, columns])
                    + matmul(backward_high[:, span], low_ref[span, columns])
                )
                result_ref[:, columns] = made if chunk + 1 == GROUP else result_ref[:, columns] + made


def column_sum(total, narrow):
    shift = LANES // 2
    while shift >= narrow:
        total = total + pltpu.roll(total, shift, 1)
        shift //= 2
    return total


def letter_sums(values_grad, choice, belongs, narrow):
    high = values_grad.astype(BF16)
    low = (values_grad - high.astype(F32)).astype(BF16)
    sums = jnp.where(belongs, matmul(choice, high) + matmul(choice, low), 0.0)
    groups = sums.shape[0] // 4
    rows = [jnp.sum(sums[groups * a : groups * a + groups], axis=0, keepdims=True) for a in range(4)]
    total = jnp.concatenate(rows, axis=0)
    return column_sum(total[:, :LANES] + total[:, LANES:], narrow)


PLACES = [(u, s) for u in range(2) for s in range(4)]


def unpack_block(receive_ref, place, samples_ref, lanes):
    stacked = []
    for u, s in PLACES:
        pieces = [
            receive_ref[16 * d + 4 * (2 * u + j) + s, place : place + 32, :] for j in range(2) for d in range(2)
        ]
        stacked.append(jnp.concatenate(pieces, axis=1))
    moved = matmul(jnp.concatenate(stacked, axis=0), swap_matrix()).astype(BF16)
    for index, (u, s) in enumerate(PLACES):
        for q in range(4):
            start = 128 * s + 32 * q
            samples_ref[start : start + 32, lanes + 128 * u : lanes + 128 * u + 128] = moved[
                32 * index : 32 * index + 32, 128 * q : 128 * q + 128
            ]


def pack_block(result_ref, lanes, send_ref, place):
    stacked = []
    for u, s in PLACES:
        pieces = [
            result_ref[128 * s + 32 * q : 128 * s + 32 * q + 32, lanes + 128 * u : lanes + 128 * u + 128]
            for q in range(4)
        ]
        stacked.append(jnp.concatenate(pieces, axis=1).astype(BF16))
    moved = matmul(jnp.concatenate(stacked, axis=0), swap_matrix()).astype(BF16)
    for index, (u, s) in enumerate(PLACES):
        for j in range(2):
            for d in range(2):
                group = 2 * j + d
                send_ref[16 * d + 4 * (2 * u + j) + s, place : place + 32, :] = moved[
                    32 * index : 32 * index + 32, 128 * group : 128 * group + 128
                ]


def unpack_taps(tails, samples_ref):
    row, lane = iota((128, 256), 0), iota((1, 256), 1)
    spot = (lane & 31) ^ ((lane >> 7) << 4)
    for d in range(2):
        tail = tails[16 * d : 16 * d + 16].reshape(128, 128).astype(BF16)
        for k in range(2):
            spread = jnp.where(row == 32 * k + spot, 1.0, 0.0).astype(BF16)
            start = 128 * (2 * d + k)
            samples_ref[start : start + 128, 512:768] = matmul(tail, spread).astype(BF16)


def pack_tails(norming, tails, result_ref, send_ref):
    quarter = iota((128, 128), 1) >> 5
    sums = column_sum(result_ref[:, 512:640], 32)
    lags = sums[0:128]
    for k in range(1, 4):
        lags = jnp.where(quarter == k, sums[128 * k : 128 * k + 128], lags)
    lags = (lags * norming).reshape(16, 8, 128).astype(BF16)
    send_ref[0:16, 64:72, :] = lags
    send_ref[16:32, 64:72, :] = lags
    line, source = iota((32, 128), 1), iota((32, 128), 0)
    letters = jnp.where(line < 64, pltpu.roll(tails[:, 0, :], 64, 1), tails[:, 1, :])
    choice = []
    for a in range(4):
        chosen = jnp.where(letters == float(a), 1.0, 0.0)
        choice.append(jnp.concatenate([jnp.where((source & 3) == s, chosen, 0.0) for s in range(4)], axis=1))
    choice = jnp.concatenate(choice, axis=0).astype(BF16)
    source = iota((128, 256), 0) & 31
    belongs = (((source >> 2) & 3) * 2 + (source >> 4)) == (iota((128, 256), 1) >> 5)
    sums = letter_sums(result_ref[:, 256:512], choice, belongs, 32) * norming
    high = sums.astype(BF16).astype(F32)
    tile = jnp.concatenate([high, sums - high], axis=0).astype(BF16)
    for index in range(32):
        send_ref[index, 72:80, :] = tile


def middle_kernel(
    norming, receive_ref, fh_ref, fl_ref, bh_hbm, bl_hbm, send_ref,
    bh_ref, bl_ref, sems, samples_ref, spectra_ref, high_ref, low_ref, result_ref,
):
    table_refs = (fh_ref, fl_ref, bh_ref, bl_ref)
    copies = copy_in([(bh_hbm, bh_ref), (bl_hbm, bl_ref)], sems)
    unpack_block(receive_ref, 0, samples_ref, 0)
    tails = receive_ref[:, 64:72, :].astype(F32)
    unpack_taps(tails, samples_ref)
    unpack_block(receive_ref, 32, samples_ref, 256)
    transforms(samples_ref, table_refs, copies, spectra_ref, high_ref, low_ref, result_ref, 32, 64)
    pack_block(result_ref, 0, send_ref, 0)
    pack_block(result_ref, 256, send_ref, 32)
    pack_tails(norming, tails, result_ref, send_ref)


def received_columns(receive_ref, place):
    stacked = []
    for m in range(8):
        pieces = [receive_ref[4 * m + d, place : place + 32, :] for d in range(4)]
        stacked.append(jnp.concatenate(pieces, axis=1))
    moved = matmul(jnp.concatenate(stacked, axis=0), swap_matrix()).astype(BF16)
    back = return_channels()
    result = []
    for u in range(4):
        columns = []
        for m in (2 * u, 2 * u + 1):
            rows = [moved[32 * m : 32 * m + 32, 128 * q : 128 * q + 128] for q in range(4)]
            columns.append(jnp.concatenate(rows, axis=0))
        result.append(matmul(jnp.concatenate(columns, axis=1), back))
    return result


def places_of(u):
    return ((slice(128 * u, 128 * u + 128), slice(0, 128)), (slice(896 - 128 * u, 1024 - 128 * u), slice(128, 256)))


def finish_kernel(receive_ref, gate_ref, upstream_ref, out_ref, hidden_ref, gated_ref, filter_ref, embedding_ref):
    for u, field in enumerate(received_columns(receive_ref, 0)):
        for there, here in places_of(u):
            out_ref[0, :, there] = (gate_ref[0, :, there].astype(F32) * field[:, here]).astype(BF16)
            gated_ref[0, :, there] = (upstream_ref[0, :, there].astype(F32) * field[:, here]).astype(BF16)
    for u, rows in enumerate(received_columns(receive_ref, 32)):
        for there, here in places_of(u):
            hidden_ref[0, :, there] = rows[:, here].astype(BF16)
    back = return_channels()
    tails = receive_ref[:, 64:80, :].astype(F32)
    stacked = [jnp.concatenate([tails[4 * m + d, 0:8, :] for d in range(4)], axis=1) for m in range(8)]
    moved = matmul(jnp.concatenate(stacked, axis=0).astype(BF16), swap_matrix())
    quarter = iota((8, 128), 1) >> 5
    for u in range(4):
        columns = []
        for m in (2 * u, 2 * u + 1):
            rows = [moved[8 * m : 8 * m + 8, 128 * k : 128 * k + 128] for k in range(4)]
            sums = tails[4 * m, 8:16, :]
            for d in range(1, 4):
                sums = jnp.where(quarter == d, tails[4 * m + d, 8:16, :], sums)
            columns.append(jnp.concatenate(rows + [sums], axis=0))
        done = matmul(jnp.concatenate(columns, axis=1).astype(BF16), back)
        for there, here in places_of(u):
            filter_ref[:, :, there] = done[0:32, here].reshape(4, 8, 128)
            embedding_ref[:, there] = done[32:36, here] + done[36:40, here]


WORK = [
    pltpu.VMEM((BLOCK, 2 * BLOCK), BF16),
    pltpu.VMEM((BLOCK, 2 * BLOCK), BF16),
    pltpu.SemaphoreType.DMA((2,)),
    pltpu.VMEM((BLOCK, 3 * COLS), BF16),
    pltpu.VMEM((2 * BLOCK, 3 * COLS), F32),
    pltpu.VMEM((2 * BLOCK, 2 * COLS + LANES), BF16),
    pltpu.VMEM((2 * BLOCK, 2 * COLS + LANES), BF16),
    pltpu.VMEM((BLOCK, 2 * COLS + LANES), F32),
]
VM = pl.BlockSpec(memory_space=pltpu.VMEM)
HBM = pl.BlockSpec(memory_space=pltpu.HBM)


def shape_of(*dims, dtype=BF16):
    return jax.ShapeDtypeStruct(dims, dtype)


def call(kernel, specs, shapes, scratch=(), mebibytes=32):
    return pl.pallas_call(
        kernel,
        in_specs=specs,
        out_shape=shapes,
        scratch_shapes=scratch,
        compiler_params=pltpu.CompilerParams(vmem_limit_bytes=mebibytes * 1024 * 1024),
    )


def in_hbm(array):
    return pltpu.with_memory_space_constraint(array, pltpu.HBM)


def placed_tables():
    fh, fl, bh, bl = tables()
    return fh, fl, in_hbm(bh), in_hbm(bl)


def exchange(array):
    return lax.all_to_all(array, ("dp", "seq"), 0, 0, tiled=True)


def packed_device(hidden, letters, gate_input, cotangent, embedding, filter_taps, norming):
    stretch = pltpu.VMEM(hidden.shape, BF16)
    sent = call(
        pack_kernel,
        [HBM] * 6,
        shape_of(32, 72, 128),
        [
            stretch,
            pltpu.VMEM(letters.shape, jnp.int32),
            stretch,
            stretch,
            pltpu.VMEM(embedding.shape, F32),
            pltpu.VMEM((2, 8, 1024), BF16),
            pltpu.SemaphoreType.DMA((6,)),
        ],
        16,
    )(*(in_hbm(array) for array in (hidden, letters, gate_input, cotangent, embedding, filter_taps)))
    here = exchange(sent)
    def kernel(*refs):
        middle_kernel(norming, *refs)

    sent = call(
        kernel,
        [VM] * 3 + [HBM] * 2,
        shape_of(32, 80, 128),
        WORK,
        24,
    )(here, *placed_tables())
    here = exchange(sent)
    shape = jax.ShapeDtypeStruct(hidden.shape, BF16)
    return call(
        finish_kernel,
        [VM] * 3,
        (shape, shape, shape, shape_of(*filter_taps.shape, dtype=F32), shape_of(*embedding.shape, dtype=F32)),
        (),
        16,
    )(here, gate_input, cotangent)


def plain_kernel(
    narrow, width, letters_ref, given_ref, fh_ref, fl_ref, bh_hbm, bl_hbm, field_ref, back_ref, lags_ref, sums_ref,
    bh_ref, bl_ref, sems, samples_ref, spectra_ref, high_ref, low_ref, result_ref,
):
    table_refs = (fh_ref, fl_ref, bh_ref, bl_ref)
    copies = copy_in([(bh_hbm, bh_ref), (bl_hbm, bl_ref)], sems)
    samples_ref[...] = given_ref[...]
    transforms(samples_ref, table_refs, copies, spectra_ref, high_ref, low_ref, result_ref, narrow, width)
    field_ref[...] = result_ref[:, 0:COLS].astype(BF16)
    back_ref[...] = result_ref[:, COLS : 2 * COLS].astype(BF16)
    lags_ref[...] = column_sum(result_ref[:, 2 * COLS :], narrow)
    letters = letters_ref[...]
    groups = COLS // narrow
    choice = jnp.concatenate(
        [jnp.where(letters == float(a), 1.0, 0.0) for a in range(4)], axis=0
    ).astype(BF16)
    shape = (4 * groups, COLS)
    belongs = (iota(shape, 0) & (groups - 1)) == iota(shape, 1) // narrow
    sums_ref[...] = letter_sums(result_ref[:, COLS : 2 * COLS], choice, belongs, narrow)


def plain_device(hidden, letters, gate_input, cotangent, embedding, filter_taps, norming):
    axes = ("dp", "seq")
    copies, stretches = lax.axis_size("dp"), lax.axis_size("seq")
    devices = copies * stretches
    stretch, channels = hidden.shape[1], hidden.shape[2]
    narrow = channels // devices
    half = narrow // 2
    blocks = stretch * stretches // BLOCK
    low = np.arange(channels // 2).reshape(devices, half)
    order = np.concatenate([low, channels - 1 - low], axis=1).reshape(-1)
    restore = np.argsort(order)
    onehot = (letters[0][:, None] == jnp.arange(embedding.shape[0], dtype=jnp.int32)[None, :]).astype(F32)
    added = jnp.dot(onehot, embedding, precision=lax.Precision.HIGHEST)
    values = (hidden[0].astype(F32) + added).astype(BF16)
    gate_wide, upstream = gate_input[0].astype(F32), cotangent[0].astype(F32)
    field_grad = (upstream * gate_wide).astype(BF16)

    def scatter(array):
        parts = jnp.take(array, order, axis=1).reshape(stretch, devices, narrow).swapaxes(0, 1)
        parts = lax.all_to_all(parts, axes, 0, 0, tiled=True)
        parts = parts.reshape(copies, blocks, BLOCK, narrow)
        return parts.transpose(2, 1, 0, 3).reshape(BLOCK, COLS)

    def gather(columns):
        parts = columns.reshape(BLOCK, blocks, copies, narrow).transpose(2, 1, 0, 3)
        parts = parts.reshape(devices, stretch, narrow)
        parts = lax.all_to_all(parts, axes, 0, 0, tiled=True)
        return jnp.take(parts.swapaxes(0, 1).reshape(stretch, channels), restore, axis=1)

    taps = lax.all_gather(filter_taps, "seq", axis=1, tiled=True).reshape(BLOCK, channels)
    mine = lax.axis_index("dp") * stretches + lax.axis_index("seq")
    own = lax.dynamic_slice_in_dim(jnp.take(taps, order, axis=1), mine * narrow, narrow, axis=1)
    mirror = jnp.roll(own, half, axis=1)
    repeats = LANES // narrow
    samples = jnp.concatenate(
        [scatter(values), scatter(field_grad), jnp.tile(own, (1, repeats)), jnp.tile(mirror, (1, repeats))], axis=1
    )
    marks = lax.all_gather(letters[0].astype(F32), axes, tiled=True)
    marks = marks.reshape(copies, blocks, BLOCK).swapaxes(0, 1).reshape(copies * blocks, BLOCK)

    def kernel(*refs):
        plain_kernel(narrow, copies * narrow, *refs)

    field, back, lags, sums = call(
        kernel,
        [VM] * 4 + [HBM] * 2,
        (
            shape_of(BLOCK, COLS),
            shape_of(BLOCK, COLS),
            shape_of(BLOCK, LANES, dtype=F32),
            shape_of(embedding.shape[0], LANES, dtype=F32),
        ),
        WORK,
    )(marks, samples, *placed_tables())
    small = jnp.concatenate([lags[:, :narrow], sums[:, :narrow]], axis=0) * norming
    small = jnp.take(lax.all_gather(small, axes, axis=1, tiled=True), restore, axis=1)
    rows = filter_taps.shape[1]
    filter_grad = lax.dynamic_slice_in_dim(
        small[:BLOCK].reshape(filter_taps.shape[0], stretch, channels), lax.axis_index("seq") * rows, rows, axis=1
    )
    field_rows, grad_rows = gather(field).astype(F32), gather(back)
    output = (gate_wide * field_rows).astype(BF16)[None]
    gate_grad = (upstream * field_rows).astype(BF16)[None]
    return output, grad_rows[None], gate_grad, filter_grad, small[BLOCK:]


def per_device(hidden, letters, gate_input, cotangent, embedding, filter_taps):
    copies, stretches = lax.axis_size("dp"), lax.axis_size("seq")
    norming = 1.0 / math.sqrt(copies * hidden.shape[0] * hidden.shape[1] * stretches)
    device = packed_device if (copies, stretches) == (2, 16) else plain_device
    return device(hidden, letters, gate_input, cotangent, embedding, filter_taps, norming)


def solution(mesh):
    return jax.shard_map(
        per_device,
        mesh=mesh,
        in_specs=(
            P("dp", "seq", None),
            P("dp", "seq"),
            P("dp", "seq", None),
            P("dp", "seq", None),
            P(),
            P(None, "seq", None),
        ),
        out_specs=(
            P("dp", "seq", None),
            P("dp", "seq", None),
            P("dp", "seq", None),
            P(None, "seq", None),
            P(),
        ),
        check_vma=False,
    )
```

time: 71.2 us -> 56 us (0.79)
  local copies, waits for them, and re-layouts: 7.68 us -> 0.03 us
  Pallas kernels: 17.2 us -> 9.85 us
    unnamed x24 -> x8, local copies, waits for them, and re-layouts: 7.68 us -> 0.03 us
    pallas_call x3, Pallas kernels: 17.2 us -> 9.85 us  [the longest x1 5.94 us: packed_device(): call(kernel, [VM] * 3 + [HBM] * 2, shape_of(32, 80, 128), WORK, 24)]
where the time goes in v1:
time: 56 us; the launch traced here: 55.8 us
  blocking collectives  45.2 us (81%)
  Pallas kernels  9.85 us (18%)
  between operations  0.68 us (1%)
    all_to_all x2, blocking collectives, exchange(): return lax.all_to_all(array, ('dp', 'seq'), 0, 0, tiled=True)  45.2 us
    pallas_call x1, Pallas kernels, packed_device(): call(kernel, [VM] * 3 + [HBM] * 2, shape_of(32, 80, 128), WORK, 24)  5.94 us
    pallas_call x1, Pallas kernels, packed_device(): call(pack_kernel, [HBM] * 6, shape_of(32, 72, 128), [stretch, pltpu.VMEM(...  2.24 us
    pallas_call x1, Pallas kernels, packed_device(): call(finish_kernel, [VM] * 3, (shape, shape, shape, shape_of(*filter_taps...  1.66 us

profile of v1, /device:TPU:0, one launch (start us, length us, event | category | flops | bytes accessed | tf_op | source)
XLA Modules:
  0.0 55.8 jit_solution(15786680085878198343)
XLA Ops:
  0.6 0.0 copy-start
  0.6 0.0 copy-start.1
  0.7 2.2 %shard_map.137 = bf16[32,72,128]{2,1,0:T(8,128)(2,1)S(1)} custom-call(bf16[1,128,1024]{2,1,0:T(8,128)(2,1)} %hidden_hbm.1, s32[1,128]{1,0:T(1,128)} %letters_hbm.1, bf16[1,128,1024]{2,1,0:T(8,128)(2,1)} %gate_ref.1, bf16[1,128,1024]{2,1,0:T(8,128)(2,1)} %upstream_ref.1, f32[4,1024]{1,0:T(4,128)} %embedding_hbm.1, bf16[4,8,1024]{2,1,0:T(8,128)(2,1)} %taps_hbm.1), custom_call_target="tpu_custom_call" | custom-call | tf_op jit(solution)/shard_map/pallas_call | solution.py:465
  2.9 24.4 %all_to_all.10.refs_0_ = bf16[32,72,128]{2,1,0:T(8,128)(2,1)S(1)} all-to-all(bf16[32,72,128]{2,1,0:T(8,128)(2,1)S(1)} %shard_map.137), channel_id=1, replica_groups=mesh['dp'=2,'seq'=16] {'dp','seq'}, dimensions={0} | all-to-all | bytes 1179648 | tf_op jit(solution)/shard_map/all_to_all | solution.py:460
  27.3 0.0 copy-done
  27.3 0.0 copy-done.1
  27.3 5.9 %shard_map.138 = bf16[32,80,128]{2,1,0:T(8,128)(2,1)S(1)} custom-call(bf16[32,72,128]{2,1,0:T(8,128)(2,1)S(1)} %all_to_all.10.refs_0_, bf16[1024,512]{1,0:T(8,128)(2,1)S(1)} %copy-done.1, bf16[1024,512]{1,0:T(8,128)(2,1)S(1)} %copy-done, bf16[512,1024]{1,0:T(8,128)(2,1)} %constant.8.clone.refs_3_, bf16[512,1024]{1,0:T(8,128)(2,1)} %constant.9.clone.refs_4_), custom_call_target="tpu_custom_call" | custom-call | tf_op jit(solution)/shard_map/pallas_call | solution.py:484
  33.3 0.0 copy-start.2
  33.3 0.0 copy-start.3
  33.3 20.8 %all_to_all.11.receive_ref = bf16[32,80,128]{2,1,0:T(8,128)(2,1)S(1)} all-to-all(bf16[32,80,128]{2,1,0:T(8,128)(2,1)S(1)} %shard_map.138), channel_id=1, replica_groups=mesh['dp'=2,'seq'=16] {'dp','seq'}, dimensions={0} | all-to-all | bytes 1310720 | tf_op jit(solution)/shard_map/all_to_all | solution.py:460
  54.1 0.0 copy-done.2
  54.1 0.0 copy-done.3
  54.1 1.7 %shard_map.139 = (bf16[1,128,1024]{2,1,0:T(8,128)(2,1)}, bf16[1,128,1024]{2,1,0:T(8,128)(2,1)}, bf16[1,128,1024]{2,1,0:T(8,128)(2,1)}, f32[4,8,1024]{2,1,0:T(8,128)}, f32[4,1024]{1,0:T(4,128)}) custom-call(bf16[32,80,128]{2,1,0:T(8,128)(2,1)S(1)} %all_to_all.11.receive_ref, bf16[1,128,1024]{2,1,0:T(8,128)(2,1)S(1)} %copy-done.2, ...), custom_call_target="tpu_custom_call" | custom-call | tf_op jit(solution)/shard_map/pallas_call | solution.py:493
Async XLA Ops:
  0.6 26.7 %copy-start = (bf16[1024,512]{1,0:T(8,128)(2,1)S(1)}, bf16[1024,512]{1,0:T(8,128)(2,1)}, u32[]{:S(2)}) copy-start(bf16[1024,512]{1,0:T(8,128)(2,1)} %constant.11.clone.refs_2_) | copy-start | bytes 3145732
  0.6 26.7 %copy-start.1 = (bf16[1024,512]{1,0:T(8,128)(2,1)S(1)}, bf16[1024,512]{1,0:T(8,128)(2,1)}, u32[]{:S(2)}) copy-start(bf16[1024,512]{1,0:T(8,128)(2,1)} %constant.10.clone.refs_1_) | copy-start | bytes 3145732
  33.3 20.8 %copy-start.2 = (bf16[1,128,1024]{2,1,0:T(8,128)(2,1)S(1)}, bf16[1,128,1024]{2,1,0:T(8,128)(2,1)}, u32[]{:S(2)}) copy-start(bf16[1,128,1024]{2,1,0:T(8,128)(2,1)} %gate_ref.1) | copy-start | bytes 786436
  33.3 20.8 %copy-start.3 = (bf16[1,128,1024]{2,1,0:T(8,128)(2,1)S(1)}, bf16[1,128,1024]{2,1,0:T(8,128)(2,1)}, u32[]{:S(2)}) copy-start(bf16[1,128,1024]{2,1,0:T(8,128)(2,1)} %upstream_ref.1) | copy-start | bytes 786436

commit v2 on v1

v2 whole, which is shorter than its diff:
```python
import math

import jax
import jax.numpy as jnp
import numpy as np
from jax import lax
from jax.experimental import pallas as pl
from jax.experimental.pallas import tpu as pltpu
from jax.sharding import PartitionSpec as P

BLOCK = 512
COLS = 256
LANES = 128
STEP = 16
CHUNK = 128
HALF_ROOT = 0.5**0.5

F32 = jnp.float32
BF16 = jnp.bfloat16


def tables():
    index = np.arange(CHUNK)[:, None]
    forward, backward = [], []
    for step, first, inputs in ((4, 0, 2), (4, 2, 2), (8, 1, 1), (8, 5, 1)):
        moment = np.arange(CHUNK * inputs)[None, :]
        phases = (step * index + first) * moment % (2 * BLOCK)
        angles = phases * (np.pi / BLOCK)
        cosines, sines = np.cos(angles), np.sin(angles)
        if inputs == 2:
            lower = -sines
            if first == 0:
                lower[0] = 1.0 - 2.0 * (moment[0] % 2)
            table = np.concatenate([cosines, lower], axis=0)
        else:
            upper = np.concatenate([cosines, sines], axis=1)
            table = np.concatenate([upper, np.concatenate([-sines, cosines], axis=1)], axis=0)
        weights = np.full((2 * CHUNK, 1), 1.0 / BLOCK)
        if first == 0:
            weights[0] = weights[CHUNK] = 0.5 / BLOCK
        forward.append(table)
        backward.append((table * weights).T)

    def halves(parts):
        table = np.concatenate(parts, axis=0)
        high = table.astype(jnp.bfloat16)
        return high, (table - high.astype(np.float64)).astype(jnp.bfloat16)

    return (*halves(forward), *halves(backward))


def iota(shape, axis):
    return lax.broadcasted_iota(jnp.int32, shape, axis)


def matmul(left, right):
    return jnp.dot(left, right, preferred_element_type=F32)


def turn(array, quarters):
    if isinstance(quarters, int) and quarters % 4 == 0:
        return array
    return pltpu.roll(array, 32 * (quarters & 3), 1)


def choose(arrays, offset, shift):
    block = ((iota(arrays[0].shape, 1) >> 5) - shift) & 3
    result = arrays[0]
    for index in range(1, 4):
        result = jnp.where(block == (index + offset) % 4, arrays[index], result)
    return result


def spread(rows, shift):
    turned = [turn(array, q + shift) for q, array in enumerate(rows)]
    return [choose(turned, d, shift) for d in range(4)]


def collect(chunks, shift):
    return [turn(choose(chunks, q, shift), -q - shift) for q in range(4)]


def owner_shift():
    return lax.axis_index("seq") & 3


def stretch_shift():
    return 2 * ((lax.axis_index("seq") >> 2) & 1) + lax.axis_index("dp")


def channel_source(lane):
    group, spot = lane >> 5, lane & 31
    return jnp.where(spot < 16, 16 * group + spot, 271 - 16 * group - spot)


def gather_channels():
    row, lane = iota((256, 256), 0), iota((1, 256), 1)
    return jnp.where(row == channel_source(lane), 1.0, 0.0).astype(BF16)


def return_channels():
    row, lane = iota((256, 1), 0), iota((256, 256), 1)
    return jnp.where(channel_source(row) == lane, 1.0, 0.0).astype(BF16)


def copy_in(pairs, sems):
    copies = [pltpu.make_async_copy(source, target, sems.at[index]) for index, (source, target) in enumerate(pairs)]
    for copy in copies:
        copy.start()
    return copies


def gathered_rows(part, gather):
    columns = []
    for u in range(4):
        pair = jnp.concatenate([part[:, 128 * u : 128 * u + 128], part[:, 896 - 128 * u : 1024 - 128 * u]], axis=1)
        both = matmul(pair, gather)
        columns += [both[:, :LANES], both[:, LANES:]]
    return columns


def send_stretch(part, gather, send_ref, place):
    shift = stretch_shift()
    for m, block in enumerate(gathered_rows(part, gather)):
        for d, chunk in enumerate(spread([block[32 * q : 32 * q + 32] for q in range(4)], shift)):
            send_ref[4 * m + d, place : place + 32, :] = chunk.astype(BF16)


def pack_kernel(
    hidden_hbm, letters_hbm, gate_hbm, upstream_hbm, embedding_hbm, taps_hbm, send_ref,
    hidden_ref, letters_ref, gate_ref, upstream_ref, embedding_ref, taps_ref, sems,
):
    copies = copy_in(
        [
            (letters_hbm, letters_ref),
            (embedding_hbm, embedding_ref),
            (hidden_hbm, hidden_ref),
            (gate_hbm, gate_ref),
            (upstream_hbm, upstream_ref),
            (taps_hbm.at[pl.ds(2 * lax.axis_index("dp"), 2)], taps_ref),
        ],
        sems,
    )
    gather = gather_channels()
    for copy in copies:
        copy.wait()
    letters = letters_ref[...].astype(F32)
    square = iota((128, 128), 0) == iota((128, 128), 1)
    letter = jnp.sum(jnp.where(square, letters, 0.0), axis=1, keepdims=True)
    added = embedding_ref[0:1, :]
    for index in range(1, 4):
        added = jnp.where(letter == float(index), embedding_ref[index : index + 1, :], added)
    send_stretch((hidden_ref[0].astype(F32) + added).astype(BF16), gather, send_ref, 0)
    send_stretch((upstream_ref[0].astype(F32) * gate_ref[0].astype(F32)).astype(BF16), gather, send_ref, 32)
    rows = gathered_rows(taps_ref[...].astype(F32).reshape(16, 1024).astype(BF16), gather)
    line = jnp.broadcast_to(letters, (8, 128))
    which, lane = iota((8, 128), 0), iota((8, 128), 1)
    shown = jnp.where(which == 0, pltpu.roll(line, 64, 1), jnp.where(which == 1, line, 0.0))
    for m, block in enumerate(rows):
        for d in range(4):
            first = turn(block[0:8], (4 - d) % 4)
            second = turn(block[8:16], (5 - d) % 4)
            piece = jnp.where(lane >= 64, shown, jnp.where(lane >= 32, second, first))
            send_ref[4 * m + d, 64:72, :] = piece.astype(BF16)


def load_pair(ref, base, start, size):
    return tuple(
        [ref[row : row + STEP, lane : lane + LANES] for lane in range(start, start + size, LANES)]
        for row in (base, base + CHUNK)
    )


def with_neighbours(pair, width, odd):
    lane = iota((STEP, LANES), 1)

    def added(here, there):
        return here - there if odd else here + there

    if width == LANES // 2:
        back, on = [], []
        for first, second in pair:
            turned, other = pltpu.roll(first, width, 1), pltpu.roll(second, width, 1)
            between = jnp.where(lane < width, turned, other)
            back.append([added(first, jnp.where(lane < width, 0.0, turned)), added(second, between)])
            on.append([added(first, between), added(second, jnp.where(lane < width, other, 0.0))])
        return tuple(back), tuple(on)
    lane = iota((STEP, COLS), 1)
    both = []
    for shift, keep in ((width, lane >= width), (COLS - width, lane < COLS - width)):
        moved = []
        for parts in pair:
            wide = jnp.concatenate(parts, axis=1)
            wide = added(wide, jnp.where(keep, pltpu.roll(wide, shift, 1), 0.0))
            moved.append([wide[:, :LANES], wide[:, LANES:]])
        both.append(tuple(moved))
    return tuple(both)


def products(first):
    real_row = iota((STEP, LANES), 0) == 0

    def settle(a, b, real, imaginary):
        if first:
            real = jnp.where(real_row, a[0] * b[0], real)
            imaginary = jnp.where(real_row, a[1] * b[1], imaginary)
        return real, imaginary

    def times(a, b):
        return settle(a, b, a[0] * b[0] - a[1] * b[1], a[0] * b[1] + a[1] * b[0])

    def times_conjugate(a, b):
        return settle(a, b, a[0] * b[0] + a[1] * b[1], a[1] * b[0] - a[0] * b[1])

    return times, times_conjugate


def plus(a, b):
    return a[0] + b[0], a[1] + b[1]


def column(pair, index):
    return pair[0][index], pair[1][index]


def store_split(high_ref, low_ref, base, start, pair):
    for row, part in ((base, 0), (base + CHUNK, 1)):
        high = pair[part].astype(BF16)
        high_ref[row : row + STEP, start : start + LANES] = high
        low_ref[row : row + STEP, start : start + LANES] = (pair[part] - high.astype(F32)).astype(BF16)


def spectra_step(spectra_ref, high_ref, low_ref, narrow, width, base):
    times, times_conjugate = products(base == 0)
    odd = base >= 4 * CHUNK
    back, on = with_neighbours(load_pair(spectra_ref, base, 0, COLS), width, odd)
    own = column(load_pair(spectra_ref, base, 2 * COLS, LANES), 0)
    mirror = column(load_pair(spectra_ref, base, 2 * COLS + LANES, LANES), 0)
    for index in range(2):
        field = plus(times(column(back, index), own), times_conjugate(column(on, index), mirror))
        store_split(high_ref, low_ref, base, LANES * index, field)
    grads = load_pair(spectra_ref, base, COLS, COLS)
    causal, ahead = None, None
    for index in range(2):
        one = times_conjugate(column(grads, index), column(back, index))
        two = times_conjugate(column(on, index), column(grads, index))
        causal = one if causal is None else plus(causal, one)
        ahead = two if ahead is None else plus(ahead, two)
    lags = plus(causal, tuple(pltpu.roll(part, narrow // 2, 1) for part in ahead))
    for row, part in ((base, lags[0]), (base + CHUNK, lags[1])):
        high = part.astype(BF16)
        high_ref[row : row + STEP, 2 * COLS : 2 * COLS + LANES] = high
        high_ref[row : row + STEP, 2 * COLS + LANES : 3 * COLS] = (part - high.astype(F32)).astype(BF16)
    back, on = with_neighbours(grads, width, odd)
    for index in range(2):
        wanted = plus(times(column(back, index), mirror), times_conjugate(column(on, index), own))
        store_split(high_ref, low_ref, base, COLS + LANES * index, wanted)


def fold(quarters):
    one, two, three, four = quarters
    between, both = HALF_ROOT * (two - four), HALF_ROOT * (two + four)
    return [one + three, two + four, one - three, two - four, one + between, -three - both, one - between, both - three]


def unfold(parts):
    between, both = HALF_ROOT * (parts[4] - parts[6]), HALF_ROOT * (parts[5] - parts[7])
    one, two = parts[0] + parts[2], parts[1] + parts[3]
    three, four = parts[0] - parts[2], parts[1] - parts[3]
    return [
        one + (parts[4] + parts[6]),
        two + (between - both),
        three - (parts[5] + parts[7]),
        four - (between + both),
    ]


def store_folded(high_ref, low_ref, row, lane, quarters):
    rows, lanes = quarters[0].shape
    for index, part in enumerate(fold(quarters)):
        start = CHUNK * index + row
        high = part.astype(BF16)
        high_ref[start : start + rows, lane : lane + lanes] = high
        low_ref[start : start + rows, lane : lane + lanes] = (part - high.astype(F32)).astype(BF16)


def transforms(inputs, table_refs, spectra_ref, high_ref, low_ref, classes_ref, result_ref, narrow, width):
    inputs_high, inputs_low = inputs
    forward_high, forward_low, backward_high, backward_low = table_refs
    chunks = BLOCK // CHUNK

    def rows_of(chunk):
        return slice(2 * CHUNK * chunk, 2 * CHUNK * (chunk + 1))

    def forward(chunk):
        rows = rows_of(chunk)
        for start in (0, 2 * COLS, COLS):
            columns = slice(start, start + COLS)
            spectra_ref[rows, columns] = (
                matmul(forward_high[rows, :], inputs_high[rows, columns])
                + matmul(forward_low[rows, :], inputs_high[rows, columns])
                + matmul(forward_high[rows, :], inputs_low[rows, columns])
            )

    def backward(chunk):
        rows = rows_of(chunk)
        for start in (COLS, 2 * COLS, 0):
            columns = slice(start, start + COLS)
            made = matmul(backward_high[rows, :], high_ref[rows, columns]) + matmul(
                backward_low[rows, :], high_ref[rows, columns]
            )
            if start < 2 * COLS:
                classes_ref[rows, columns] = made + matmul(backward_high[rows, :], low_ref[rows, columns])
            else:
                classes_ref[rows, start : start + LANES] = made[:, :LANES] + made[:, LANES:]

    forward(0)
    for chunk in range(chunks):
        if chunk + 1 < chunks:
            forward(chunk + 1)
        for base in range(2 * CHUNK * chunk, 2 * CHUNK * chunk + CHUNK, STEP):
            spectra_step(spectra_ref, high_ref, low_ref, narrow, width, base)
        backward(chunk)
    for lane in (COLS, COLS + LANES, 2 * COLS, 0, LANES):
        lanes = slice(lane, lane + LANES)
        for row in range(0, CHUNK, 32):
            parts = [classes_ref[CHUNK * index + row : CHUNK * index + row + 32, lanes] for index in range(8)]
            for quarter, part in enumerate(unfold(parts)):
                result_ref[CHUNK * quarter + row : CHUNK * quarter + row + 32, lanes] = part


def column_sum(total, narrow):
    shift = LANES // 2
    while shift >= narrow:
        total = total + pltpu.roll(total, shift, 1)
        shift //= 2
    return total


def letter_sums(values_grad, choice, belongs, narrow):
    high = values_grad.astype(BF16)
    low = (values_grad - high.astype(F32)).astype(BF16)
    sums = jnp.where(belongs, matmul(choice, high) + matmul(choice, low), 0.0)
    groups = sums.shape[0] // 4
    rows = [jnp.sum(sums[groups * a : groups * a + groups], axis=0, keepdims=True) for a in range(4)]
    total = jnp.concatenate(rows, axis=0)
    return column_sum(total[:, :LANES] + total[:, LANES:], narrow)


PLACES = [(u, s) for u in range(2) for s in range(4)]


def unpack_block(receive_ref, place, high_ref, low_ref, lanes):
    shift = owner_shift()
    for u in range(2):
        stretches = []
        for s in range(4):
            chunks = [
                receive_ref[16 * d + 4 * (2 * u + j) + s, place : place + 32, :].astype(F32)
                for j in range(2)
                for d in range(2)
            ]
            stretches.append(collect(chunks, shift))
        for q in range(4):
            store_folded(high_ref, low_ref, 32 * q, lanes + 128 * u, [rows[q] for rows in stretches])


def pack_block(result_ref, lanes, send_ref, place):
    shift = owner_shift()
    for u, s in PLACES:
        rows = [
            result_ref[128 * s + 32 * q : 128 * s + 32 * q + 32, lanes + 128 * u : lanes + 128 * u + 128]
            for q in range(4)
        ]
        for group, chunk in enumerate(spread(rows, shift)):
            j, d = group // 2, group % 2
            send_ref[16 * d + 4 * (2 * u + j) + s, place : place + 32, :] = chunk.astype(BF16)


def unpack_taps(tails, high_ref, low_ref):
    row, lane = iota((128, 256), 0), iota((1, 256), 1)
    spot = (lane & 31) ^ ((lane >> 7) << 4)
    quarters = []
    for d in range(2):
        tail = tails[16 * d : 16 * d + 16].reshape(128, 128).astype(BF16)
        for k in range(2):
            quarters.append(matmul(tail, jnp.where(row == 32 * k + spot, 1.0, 0.0).astype(BF16)))
    store_folded(high_ref, low_ref, 0, 512, quarters)


def pack_tails(norming, tails, result_ref, send_ref):
    quarter = ((iota((128, 128), 1) >> 5) - lax.axis_index("seq")) & 3
    sums = column_sum(result_ref[:, 512:640], 32)
    lags = sums[0:128]
    for k in range(1, 4):
        lags = jnp.where(quarter == k, sums[128 * k : 128 * k + 128], lags)
    lags = (lags * norming).reshape(16, 8, 128).astype(BF16)
    send_ref[0:16, 64:72, :] = lags
    send_ref[16:32, 64:72, :] = lags
    line, source = iota((32, 128), 1), iota((32, 128), 0)
    letters = jnp.where(line < 64, pltpu.roll(tails[:, 0, :], 64, 1), tails[:, 1, :])
    choice = []
    for a in range(4):
        chosen = jnp.where(letters == float(a), 1.0, 0.0)
        choice.append(jnp.concatenate([jnp.where((source & 3) == s, chosen, 0.0) for s in range(4)], axis=1))
    choice = jnp.concatenate(choice, axis=0).astype(BF16)
    source = iota((128, 256), 0) & 31
    belongs = (((source >> 2) & 3) * 2 + (source >> 4)) == (iota((128, 256), 1) >> 5)
    sums = letter_sums(result_ref[:, 256:512], choice, belongs, 32) * norming
    high = sums.astype(BF16).astype(F32)
    tile = jnp.concatenate([high, sums - high], axis=0).astype(BF16)
    for index in range(32):
        send_ref[index, 72:80, :] = tile


def middle_kernel(
    norming, receive_ref, fh_ref, fl_ref, bh_ref, bl_ref, send_ref,
    inputs_high_ref, inputs_low_ref, spectra_ref, high_ref, low_ref, classes_ref, result_ref,
):
    tails = receive_ref[:, 64:72, :].astype(F32)
    unpack_taps(tails, inputs_high_ref, inputs_low_ref)
    unpack_block(receive_ref, 0, inputs_high_ref, inputs_low_ref, 0)
    unpack_block(receive_ref, 32, inputs_high_ref, inputs_low_ref, 256)
    transforms(
        (inputs_high_ref, inputs_low_ref), (fh_ref, fl_ref, bh_ref, bl_ref),
        spectra_ref, high_ref, low_ref, classes_ref, result_ref, 32, 64,
    )
    pack_tails(norming, tails, result_ref, send_ref)
    pack_block(result_ref, 256, send_ref, 32)
    pack_block(result_ref, 0, send_ref, 0)


def received_columns(receive_ref, place, back):
    shift = stretch_shift()
    result = []
    for u in range(4):
        columns = []
        for m in (2 * u, 2 * u + 1):
            chunks = [receive_ref[4 * m + d, place : place + 32, :].astype(F32) for d in range(4)]
            columns.append(jnp.concatenate(collect(chunks, shift), axis=0).astype(BF16))
        result.append(matmul(jnp.concatenate(columns, axis=1), back))
    return result


def places_of(u):
    return ((slice(128 * u, 128 * u + 128), slice(0, 128)), (slice(896 - 128 * u, 1024 - 128 * u), slice(128, 256)))


def finish_kernel(receive_ref, gate_ref, upstream_ref, out_ref, hidden_ref, gated_ref, filter_ref, embedding_ref):
    back = return_channels()
    for u, field in enumerate(received_columns(receive_ref, 0, back)):
        for there, here in places_of(u):
            out_ref[0, :, there] = (gate_ref[0, :, there].astype(F32) * field[:, here]).astype(BF16)
            gated_ref[0, :, there] = (upstream_ref[0, :, there].astype(F32) * field[:, here]).astype(BF16)
    for u, rows in enumerate(received_columns(receive_ref, 32, back)):
        for there, here in places_of(u):
            hidden_ref[0, :, there] = rows[:, here].astype(BF16)
    tails = receive_ref[:, 64:80, :].astype(F32)
    for u in range(4):
        columns = []
        for m in (2 * u, 2 * u + 1):
            rows = collect([tails[4 * m + d, 0:8, :] for d in range(4)], 0)
            sums = choose([tails[4 * m + d, 8:16, :] for d in range(4)], 0, 0)
            columns.append(jnp.concatenate(rows + [sums], axis=0))
        done = matmul(jnp.concatenate(columns, axis=1).astype(BF16), back)
        for there, here in places_of(u):
            filter_ref[:, :, there] = done[0:32, here].reshape(4, 8, 128)
            embedding_ref[:, there] = done[32:36, here] + done[36:40, here]


WORK = [
    pltpu.VMEM((2 * BLOCK, 3 * COLS), BF16),
    pltpu.VMEM((2 * BLOCK, 3 * COLS), BF16),
    pltpu.VMEM((2 * BLOCK, 3 * COLS), F32),
    pltpu.VMEM((2 * BLOCK, 3 * COLS), BF16),
    pltpu.VMEM((2 * BLOCK, 2 * COLS), BF16),
    pltpu.VMEM((2 * BLOCK, 2 * COLS + LANES), F32),
    pltpu.VMEM((BLOCK, 2 * COLS + LANES), F32),
]
VM = pl.BlockSpec(memory_space=pltpu.VMEM)
HBM = pl.BlockSpec(memory_space=pltpu.HBM)


def shape_of(*dims, dtype=BF16):
    return jax.ShapeDtypeStruct(dims, dtype)


def call(kernel, specs, shapes, scratch=(), mebibytes=32):
    return pl.pallas_call(
        kernel,
        in_specs=specs,
        out_shape=shapes,
        scratch_shapes=scratch,
        compiler_params=pltpu.CompilerParams(vmem_limit_bytes=mebibytes * 1024 * 1024),
    )


def in_hbm(array):
    return pltpu.with_memory_space_constraint(array, pltpu.HBM)


def exchange(array):
    return lax.all_to_all(array, ("dp", "seq"), 0, 0, tiled=True)


def packed_device(hidden, letters, gate_input, cotangent, embedding, filter_taps, norming):
    stretch = pltpu.VMEM(hidden.shape, BF16)
    sent = call(
        pack_kernel,
        [HBM] * 6,
        shape_of(32, 72, 128),
        [
            stretch,
            pltpu.VMEM(letters.shape, jnp.int32),
            stretch,
            stretch,
            pltpu.VMEM(embedding.shape, F32),
            pltpu.VMEM((2, 8, 1024), BF16),
            pltpu.SemaphoreType.DMA((6,)),
        ],
        16,
    )(*(in_hbm(array) for array in (hidden, letters, gate_input, cotangent, embedding, filter_taps)))
    here = exchange(sent)
    def kernel(*refs):
        middle_kernel(norming, *refs)

    sent = call(
        kernel,
        [VM] * 5,
        shape_of(32, 80, 128),
        WORK,
        24,
    )(here, *tables())
    here = exchange(sent)
    shape = jax.ShapeDtypeStruct(hidden.shape, BF16)
    return call(
        finish_kernel,
        [VM] * 3,
        (shape, shape, shape, shape_of(*filter_taps.shape, dtype=F32), shape_of(*embedding.shape, dtype=F32)),
        (),
        16,
    )(here, gate_input, cotangent)


def plain_kernel(
    narrow, width, letters_ref, samples_ref, fh_ref, fl_ref, bh_ref, bl_ref, field_ref, back_ref, lags_ref, sums_ref,
    inputs_high_ref, inputs_low_ref, spectra_ref, high_ref, low_ref, classes_ref, result_ref,
):
    for lane in range(0, 3 * COLS, LANES):
        quarters = [samples_ref[row : row + CHUNK, lane : lane + LANES].astype(F32) for row in range(0, BLOCK, CHUNK)]
        store_folded(inputs_high_ref, inputs_low_ref, 0, lane, quarters)
    transforms(
        (inputs_high_ref, inputs_low_ref), (fh_ref, fl_ref, bh_ref, bl_ref),
        spectra_ref, high_ref, low_ref, classes_ref, result_ref, narrow, width,
    )
    field_ref[...] = result_ref[:, 0:COLS].astype(BF16)
    back_ref[...] = result_ref[:, COLS : 2 * COLS].astype(BF16)
    lags_ref[...] = column_sum(result_ref[:, 2 * COLS :], narrow)
    letters = letters_ref[...]
    groups = COLS // narrow
    choice = jnp.concatenate(
        [jnp.where(letters == float(a), 1.0, 0.0) for a in range(4)], axis=0
    ).astype(BF16)
    shape = (4 * groups, COLS)
    belongs = (iota(shape, 0) & (groups - 1)) == iota(shape, 1) // narrow
    sums_ref[...] = letter_sums(result_ref[:, COLS : 2 * COLS], choice, belongs, narrow)


def plain_device(hidden, letters, gate_input, cotangent, embedding, filter_taps, norming):
    axes = ("dp", "seq")
    copies, stretches = lax.axis_size("dp"), lax.axis_size("seq")
    devices = copies * stretches
    stretch, channels = hidden.shape[1], hidden.shape[2]
    narrow = channels // devices
    half = narrow // 2
    blocks = stretch * stretches // BLOCK
    low = np.arange(channels // 2).reshape(devices, half)
    order = np.concatenate([low, channels - 1 - low], axis=1).reshape(-1)
    restore = np.argsort(order)
    onehot = (letters[0][:, None] == jnp.arange(embedding.shape[0], dtype=jnp.int32)[None, :]).astype(F32)
    added = jnp.dot(onehot, embedding, precision=lax.Precision.HIGHEST)
    values = (hidden[0].astype(F32) + added).astype(BF16)
    gate_wide, upstream = gate_input[0].astype(F32), cotangent[0].astype(F32)
    field_grad = (upstream * gate_wide).astype(BF16)

    def scatter(array):
        parts = jnp.take(array, order, axis=1).reshape(stretch, devices, narrow).swapaxes(0, 1)
        parts = lax.all_to_all(parts, axes, 0, 0, tiled=True)
        parts = parts.reshape(copies, blocks, BLOCK, narrow)
        return parts.transpose(2, 1, 0, 3).reshape(BLOCK, COLS)

    def gather(columns):
        parts = columns.reshape(BLOCK, blocks, copies, narrow).transpose(2, 1, 0, 3)
        parts = parts.reshape(devices, stretch, narrow)
        parts = lax.all_to_all(parts, axes, 0, 0, tiled=True)
        return jnp.take(parts.swapaxes(0, 1).reshape(stretch, channels), restore, axis=1)

    taps = lax.all_gather(filter_taps, "seq", axis=1, tiled=True).reshape(BLOCK, channels)
    mine = lax.axis_index("dp") * stretches + lax.axis_index("seq")
    own = lax.dynamic_slice_in_dim(jnp.take(taps, order, axis=1), mine * narrow, narrow, axis=1)
    mirror = jnp.roll(own, half, axis=1)
    repeats = LANES // narrow
    samples = jnp.concatenate(
        [scatter(values), scatter(field_grad), jnp.tile(own, (1, repeats)), jnp.tile(mirror, (1, repeats))], axis=1
    )
    marks = lax.all_gather(letters[0].astype(F32), axes, tiled=True)
    marks = marks.reshape(copies, blocks, BLOCK).swapaxes(0, 1).reshape(copies * blocks, BLOCK)

    def kernel(*refs):
        plain_kernel(narrow, copies * narrow, *refs)

    field, back, lags, sums = call(
        kernel,
        [VM] * 6,
        (
            shape_of(BLOCK, COLS),
            shape_of(BLOCK, COLS),
            shape_of(BLOCK, LANES, dtype=F32),
            shape_of(embedding.shape[0], LANES, dtype=F32),
        ),
        WORK,
    )(marks, samples, *tables())
    small = jnp.concatenate([lags[:, :narrow], sums[:, :narrow]], axis=0) * norming
    small = jnp.take(lax.all_gather(small, axes, axis=1, tiled=True), restore, axis=1)
    rows = filter_taps.shape[1]
    filter_grad = lax.dynamic_slice_in_dim(
        small[:BLOCK].reshape(filter_taps.shape[0], stretch, channels), lax.axis_index("seq") * rows, rows, axis=1
    )
    field_rows, grad_rows = gather(field).astype(F32), gather(back)
    output = (gate_wide * field_rows).astype(BF16)[None]
    gate_grad = (upstream * field_rows).astype(BF16)[None]
    return output, grad_rows[None], gate_grad, filter_grad, small[BLOCK:]


def per_device(hidden, letters, gate_input, cotangent, embedding, filter_taps):
    copies, stretches = lax.axis_size("dp"), lax.axis_size("seq")
    norming = 1.0 / math.sqrt(copies * hidden.shape[0] * hidden.shape[1] * stretches)
    device = packed_device if (copies, stretches) == (2, 16) else plain_device
    return device(hidden, letters, gate_input, cotangent, embedding, filter_taps, norming)


def solution(mesh):
    return jax.shard_map(
        per_device,
        mesh=mesh,
        in_specs=(
            P("dp", "seq", None),
            P("dp", "seq"),
            P("dp", "seq", None),
            P("dp", "seq", None),
            P(),
            P(None, "seq", None),
        ),
        out_specs=(
            P("dp", "seq", None),
            P("dp", "seq", None),
            P("dp", "seq", None),
            P(None, "seq", None),
            P(),
        ),
        check_vma=False,
    )
```

time: 56 us -> 54 us (0.964)
  Pallas kernels: 9.85 us -> 7.83 us
    pallas_call x1, Pallas kernels: 5.94 us -> 4.57 us  [packed_device(): call(kernel, [VM] * 5, shape_of(32, 80, 128), WORK, 24)(here, *tables())]
where the time goes in v2:
time: 54 us; the launch traced here: 53.8 us
  blocking collectives  45.2 us (84%)
  Pallas kernels  7.83 us (14%)
  between operations  0.71 us (1%)
    all_to_all x2, blocking collectives, exchange(): return lax.all_to_all(array, ('dp', 'seq'), 0, 0, tiled=True)  45.2 us
    pallas_call x1, Pallas kernels, packed_device(): call(kernel, [VM] * 5, shape_of(32, 80, 128), WORK, 24)(here, *tables())  4.57 us
    pallas_call x1, Pallas kernels, packed_device(): call(pack_kernel, [HBM] * 6, shape_of(32, 72, 128), [stretch, pltpu.VMEM(...  1.87 us
    pallas_call x1, Pallas kernels, packed_device(): call(finish_kernel, [VM] * 3, (shape, shape, shape, shape_of(*filter_taps...  1.39 us

profile of v2, /device:TPU:0, one launch (start us, length us, event | category | flops | bytes accessed | tf_op | source)
XLA Modules:
  0.0 53.8 jit_solution(8967369317611600004)
XLA Ops:
  0.6 0.0 copy-start.4
  0.6 0.0 copy-start.5
  0.7 1.9 %shard_map.137 = bf16[32,72,128]{2,1,0:T(8,128)(2,1)S(1)} custom-call(bf16[1,128,1024]{2,1,0:T(8,128)(2,1)} %hidden_hbm.1, s32[1,128]{1,0:T(1,128)} %letters_hbm.1, bf16[1,128,1024]{2,1,0:T(8,128)(2,1)} %gate_ref.1, bf16[1,128,1024]{2,1,0:T(8,128)(2,1)} %upstream_ref.1, f32[4,1024]{1,0:T(4,128)} %embedding_hbm.1, bf16[4,8,1024]{2,1,0:T(8,128)(2,1)} %taps_hbm.1), custom_call_target="tpu_custom_call" | custom-call | tf_op jit(solution)/shard_map/pallas_call | solution.py:508
  2.5 0.0 copy-start.2
  2.5 0.0 copy-start.3
  2.6 24.4 %all_to_all.10.refs_0_ = bf16[32,72,128]{2,1,0:T(8,128)(2,1)S(1)} all-to-all(bf16[32,72,128]{2,1,0:T(8,128)(2,1)S(1)} %shard_map.137), channel_id=1, replica_groups=mesh['dp'=2,'seq'=16] {'dp','seq'}, dimensions={0} | all-to-all | bytes 1179648 | tf_op jit(solution)/shard_map/all_to_all | solution.py:503
  27.0 0.0 copy-done.4
  27.0 0.0 copy-done.5
  27.0 0.0 copy-done.2
  27.0 0.0 copy-done.3
  27.0 4.6 %shard_map.138 = bf16[32,80,128]{2,1,0:T(8,128)(2,1)S(1)} custom-call(bf16[32,72,128]{2,1,0:T(8,128)(2,1)S(1)} %all_to_all.10.refs_0_, bf16[1024,256]{1,0:T(8,128)(2,1)S(1)} %copy-done.5, bf16[1024,256]{1,0:T(8,128)(2,1)S(1)} %copy-done.4, bf16[1024,256]{1,0:T(8,128)(2,1)S(1)} %copy-done.3, bf16[1024,256]{1,0:T(8,128)(2,1)S(1)} %copy-done.2), custom_call_target="tpu_custom_call" | custom-call | tf_op jit(solution)/shard_map/pallas_call | solution.py:527
  31.6 0.0 copy-start
  31.6 0.0 copy-start.1
  31.6 20.8 %all_to_all.11.receive_ref = bf16[32,80,128]{2,1,0:T(8,128)(2,1)S(1)} all-to-all(bf16[32,80,128]{2,1,0:T(8,128)(2,1)S(1)} %shard_map.138), channel_id=1, replica_groups=mesh['dp'=2,'seq'=16] {'dp','seq'}, dimensions={0} | all-to-all | bytes 1310720 | tf_op jit(solution)/shard_map/all_to_all | solution.py:503
  52.4 0.0 copy-done
  52.4 0.0 copy-done.1
  52.4 1.4 %shard_map.139 = (bf16[1,128,1024]{2,1,0:T(8,128)(2,1)}, bf16[1,128,1024]{2,1,0:T(8,128)(2,1)}, bf16[1,128,1024]{2,1,0:T(8,128)(2,1)}, f32[4,8,1024]{2,1,0:T(8,128)}, f32[4,1024]{1,0:T(4,128)}) custom-call(bf16[32,80,128]{2,1,0:T(8,128)(2,1)S(1)} %all_to_all.11.receive_ref, bf16[1,128,1024]{2,1,0:T(8,128)(2,1)S(1)} %copy-done, ...), custom_call_target="tpu_custom_call" | custom-call | tf_op jit(solution)/shard_map/pallas_call | solution.py:536
Async XLA Ops:
  0.6 26.3 %copy-start.4 = (bf16[1024,256]{1,0:T(8,128)(2,1)S(1)}, bf16[1024,256]{1,0:T(8,128)(2,1)}, u32[]{:S(2)}) copy-start(bf16[1024,256]{1,0:T(8,128)(2,1)} %constant.9.clone.refs_2_) | copy-start | bytes 1572868
  0.6 26.3 %copy-start.5 = (bf16[1024,256]{1,0:T(8,128)(2,1)S(1)}, bf16[1024,256]{1,0:T(8,128)(2,1)}, u32[]{:S(2)}) copy-start(bf16[1024,256]{1,0:T(8,128)(2,1)} %constant.8.clone.refs_1_) | copy-start | bytes 1572868
  2.5 24.4 %copy-start.2 = (bf16[1024,256]{1,0:T(8,128)(2,1)S(1)}, bf16[1024,256]{1,0:T(8,128)(2,1)}, u32[]{:S(2)}) copy-start(bf16[1024,256]{1,0:T(8,128)(2,1)} %constant.11.clone.refs_4_) | copy-start | bytes 1572868
  2.5 24.4 %copy-start.3 = (bf16[1024,256]{1,0:T(8,128)(2,1)S(1)}, bf16[1024,256]{1,0:T(8,128)(2,1)}, u32[]{:S(2)}) copy-start(bf16[1024,256]{1,0:T(8,128)(2,1)} %constant.10.clone.refs_3_) | copy-start | bytes 1572868
  31.6 20.8 %copy-start = (bf16[1,128,1024]{2,1,0:T(8,128)(2,1)S(1)}, bf16[1,128,1024]{2,1,0:T(8,128)(2,1)}, u32[]{:S(2)}) copy-start(bf16[1,128,1024]{2,1,0:T(8,128)(2,1)} %gate_ref.1) | copy-start | bytes 786436
  31.6 20.8 %copy-start.1 = (bf16[1,128,1024]{2,1,0:T(8,128)(2,1)S(1)}, bf16[1,128,1024]{2,1,0:T(8,128)(2,1)}, u32[]{:S(2)}) copy-start(bf16[1,128,1024]{2,1,0:T(8,128)(2,1)} %upstream_ref.1) | copy-start | bytes 786436

commit v3 on v2

--- a/solution.py
+++ b/solution.py
@@ -14,6 +14,7 @@
 STEP = 16
 CHUNK = 128
 HALF_ROOT = 0.5**0.5
+CHUNK_ROWS = 74
 
 F32 = jnp.float32
 BF16 = jnp.bfloat16
@@ -365,7 +366,16 @@
             store_folded(high_ref, low_ref, 32 * q, lanes + 128 * u, [rows[q] for rows in stretches])
 
 
-def pack_block(result_ref, lanes, send_ref, place):
+def put(send_ref, index, pair, rows):
+    start = CHUNK_ROWS * index + 2 * pair
+    send_ref[start : start + rows.shape[0], :] = rows.astype(BF16)
+
+
+def take(receive_ref, index, pair, count):
+    return receive_ref[index, pair : pair + count].reshape(2 * count, LANES).astype(F32)
+
+
+def pack_block(result_ref, lanes, send_ref, pair):
     shift = owner_shift()
     for u, s in PLACES:
         rows = [
@@ -374,7 +384,7 @@
         ]
         for group, chunk in enumerate(spread(rows, shift)):
             j, d = group // 2, group % 2
-            send_ref[16 * d + 4 * (2 * u + j) + s, place : place + 32, :] = chunk.astype(BF16)
+            put(send_ref, 16 * d + 4 * (2 * u + j) + s, pair, chunk)
 
 
 def unpack_taps(tails, high_ref, low_ref):
@@ -394,9 +404,10 @@
     lags = sums[0:128]
     for k in range(1, 4):
         lags = jnp.where(quarter == k, sums[128 * k : 128 * k + 128], lags)
-    lags = (lags * norming).reshape(16, 8, 128).astype(BF16)
-    send_ref[0:16, 64:72, :] = lags
-    send_ref[16:32, 64:72, :] = lags
+    lags = lags * norming
+    for index in range(16):
+        put(send_ref, index, 32, lags[8 * index : 8 * index + 8])
+        put(send_ref, 16 + index, 32, lags[8 * index : 8 * index + 8])
     line, source = iota((32, 128), 1), iota((32, 128), 0)
     letters = jnp.where(line < 64, pltpu.roll(tails[:, 0, :], 64, 1), tails[:, 1, :])
     choice = []
@@ -407,10 +418,11 @@
     source = iota((128, 256), 0) & 31
     belongs = (((source >> 2) & 3) * 2 + (source >> 4)) == (iota((128, 256), 1) >> 5)
     sums = letter_sums(result_ref[:, 256:512], choice, belongs, 32) * norming
+    sums = choose([sums[a : a + 1] for a in range(4)], 0, owner_shift())
     high = sums.astype(BF16).astype(F32)
-    tile = jnp.concatenate([high, sums - high], axis=0).astype(BF16)
+    tile = jnp.concatenate([high, sums - high], axis=0)
     for index in range(32):
-        send_ref[index, 72:80, :] = tile
+        put(send_ref, index, 36, tile)
 
 
 def middle_kernel(
@@ -426,17 +438,17 @@
         spectra_ref, high_ref, low_ref, classes_ref, result_ref, 32, 64,
     )
     pack_tails(norming, tails, result_ref, send_ref)
-    pack_block(result_ref, 256, send_ref, 32)
+    pack_block(result_ref, 256, send_ref, 16)
     pack_block(result_ref, 0, send_ref, 0)
 
 
-def received_columns(receive_ref, place, back):
+def received_columns(receive_ref, pair, back):
     shift = stretch_shift()
     result = []
     for u in range(4):
         columns = []
         for m in (2 * u, 2 * u + 1):
-            chunks = [receive_ref[4 * m + d, place : place + 32, :].astype(F32) for d in range(4)]
+            chunks = [take(receive_ref, 4 * m + d, pair, 16) for d in range(4)]
             columns.append(jnp.concatenate(collect(chunks, shift), axis=0).astype(BF16))
         result.append(matmul(jnp.concatenate(columns, axis=1), back))
     return result
@@ -452,20 +464,30 @@
         for there, here in places_of(u):
             out_ref[0, :, there] = (gate_ref[0, :, there].astype(F32) * field[:, here]).astype(BF16)
             gated_ref[0, :, there] = (upstream_ref[0, :, there].astype(F32) * field[:, here]).astype(BF16)
-    for u, rows in enumerate(received_columns(receive_ref, 32, back)):
+    for u, rows in enumerate(received_columns(receive_ref, 16, back)):
         for there, here in places_of(u):
             hidden_ref[0, :, there] = rows[:, here].astype(BF16)
-    tails = receive_ref[:, 64:80, :].astype(F32)
     for u in range(4):
         columns = []
         for m in (2 * u, 2 * u + 1):
-            rows = collect([tails[4 * m + d, 0:8, :] for d in range(4)], 0)
-            sums = choose([tails[4 * m + d, 8:16, :] for d in range(4)], 0, 0)
-            columns.append(jnp.concatenate(rows + [sums], axis=0))
+            columns.append(jnp.concatenate(collect([take(receive_ref, 4 * m + d, 32, 4) for d in range(4)], 0), axis=0))
         done = matmul(jnp.concatenate(columns, axis=1).astype(BF16), back)
         for there, here in places_of(u):
-            filter_ref[:, :, there] = done[0:32, here].reshape(4, 8, 128)
-            embedding_ref[:, there] = done[32:36, here] + done[36:40, here]
+            filter_ref[:, :, there] = done[:, here].reshape(4, 8, 128)
+    sums = collect(
+        [jnp.concatenate([take(receive_ref, 4 * m + d, 36, 1) for m in range(8)], axis=0) for d in range(4)], 0
+    )
+    rows = []
+    for term in range(2):
+        for u in range(4):
+            for total in sums:
+                first, second = total[4 * u + term : 4 * u + term + 1], total[4 * u + 2 + term : 4 * u + 3 + term]
+                rows.append(jnp.concatenate([first, second], axis=1))
+    done = matmul(jnp.concatenate(rows, axis=0).astype(BF16), back)
+    done = done[0:16] + done[16:32]
+    for u in range(4):
+        for there, here in places_of(u):
+            embedding_ref[:, there] = done[4 * u : 4 * u + 4, here]
 
 
 WORK = [
@@ -527,11 +549,11 @@
     sent = call(
         kernel,
         [VM] * 5,
-        shape_of(32, 80, 128),
+        shape_of(32 * CHUNK_ROWS, LANES),
         WORK,
         24,
     )(here, *tables())
-    here = exchange(sent)
+    here = exchange(sent.reshape(32, CHUNK_ROWS // 2, 2, LANES))
     shape = jax.ShapeDtypeStruct(hidden.shape, BF16)
     return call(
         finish_kernel,

time: 54 us -> 53.3 us (0.987)
  blocking collectives: 45.2 us -> 44.1 us
    all_to_all x2, blocking collectives: 45.2 us -> 44.1 us  [exchange(): return lax.all_to_all(array, ('dp', 'seq'), 0, 0, tiled=True)]
where the time goes in v3:
time: 53.3 us; the launch traced here: 53.1 us
  blocking collectives  44.1 us (83%)
  Pallas kernels  8.21 us (15%)
  between operations  0.71 us (1%)
    all_to_all x2, blocking collectives, exchange(): return lax.all_to_all(array, ('dp', 'seq'), 0, 0, tiled=True)  44.1 us
    pallas_call x1, Pallas kernels, packed_device(): call(kernel, [VM] * 5, shape_of(32 * CHUNK_ROWS, LANES), WORK, 24)  4.61 us
    pallas_call x1, Pallas kernels, packed_device(): call(pack_kernel, [HBM] * 6, shape_of(32, 72, 128), [stretch, pltpu.VMEM(...  1.87 us
    pallas_call x1, Pallas kernels, packed_device(): call(finish_kernel, [VM] * 3, (shape, shape, shape, shape_of(*filter_taps...  1.73 us

profile of v3, /device:TPU:0, one launch (start us, length us, event | category | flops | bytes accessed | tf_op | source)
XLA Modules:
  0.0 53.1 jit_solution(17358674659855633942)
XLA Ops:
  0.6 0.0 copy-start.4
  0.6 0.0 copy-start.5
  0.7 1.9 %shard_map.137 = bf16[32,72,128]{2,1,0:T(8,128)(2,1)S(1)} custom-call(bf16[1,128,1024]{2,1,0:T(8,128)(2,1)} %hidden_hbm.1, s32[1,128]{1,0:T(1,128)} %letters_hbm.1, bf16[1,128,1024]{2,1,0:T(8,128)(2,1)} %gate_ref.1, bf16[1,128,1024]{2,1,0:T(8,128)(2,1)} %upstream_ref.1, f32[4,1024]{1,0:T(4,128)} %embedding_hbm.1, bf16[4,8,1024]{2,1,0:T(8,128)(2,1)} %taps_hbm.1), custom_call_target="tpu_custom_call" | custom-call | tf_op jit(solution)/shard_map/pallas_call | solution.py:530
  2.5 0.0 copy-start.2
  2.5 0.0 copy-start.3
  2.6 24.4 %all_to_all.10.refs_0_ = bf16[32,72,128]{2,1,0:T(8,128)(2,1)S(1)} all-to-all(bf16[32,72,128]{2,1,0:T(8,128)(2,1)S(1)} %shard_map.137), channel_id=1, replica_groups=mesh['dp'=2,'seq'=16] {'dp','seq'}, dimensions={0} | all-to-all | bytes 1179648 | tf_op jit(solution)/shard_map/all_to_all | solution.py:525
  27.0 0.0 copy-done.4
  27.0 0.0 copy-done.5
  27.0 0.0 copy-done.2
  27.0 0.0 copy-done.3
  27.0 4.6 %shard_map.138 = bf16[2368,128]{1,0:T(8,128)(2,1)S(1)} custom-call(bf16[32,72,128]{2,1,0:T(8,128)(2,1)S(1)} %all_to_all.10.refs_0_, bf16[1024,256]{1,0:T(8,128)(2,1)S(1)} %copy-done.5, bf16[1024,256]{1,0:T(8,128)(2,1)S(1)} %copy-done.4, bf16[1024,256]{1,0:T(8,128)(2,1)S(1)} %copy-done.3, bf16[1024,256]{1,0:T(8,128)(2,1)S(1)} %copy-done.2), custom_call_target="tpu_custom_call" | custom-call | tf_op jit(solution)/shard_map/pallas_call | solution.py:549
  31.6 0.0 copy-start
  31.6 0.0 copy-start.1
  31.6 19.7 %all_to_all.11.receive_ref = bf16[32,37,2,128]{3,2,1,0:T(2,128)(2,1)S(1)} all-to-all(bf16[32,37,2,128]{3,2,1,0:T(2,128)(2,1)S(1)} %bitcast.1), channel_id=1, replica_groups=mesh['dp'=2,'seq'=16] {'dp','seq'}, dimensions={0} | all-to-all | bytes 1212416 | tf_op jit(solution)/shard_map/all_to_all | solution.py:525
  51.4 0.0 copy-done
  51.4 0.0 copy-done.1
  51.4 1.7 %shard_map.139 = (bf16[1,128,1024]{2,1,0:T(8,128)(2,1)}, bf16[1,128,1024]{2,1,0:T(8,128)(2,1)}, bf16[1,128,1024]{2,1,0:T(8,128)(2,1)}, f32[4,8,1024]{2,1,0:T(8,128)}, f32[4,1024]{1,0:T(4,128)}) custom-call(bf16[32,37,2,128]{3,2,1,0:T(2,128)(2,1)S(1)} %all_to_all.11.receive_ref, bf16[1,128,1024]{2,1,0:T(8,128)(2,1)S(1)} %copy-done, ...), custom_call_target="tpu_custom_call" | custom-call | tf_op jit(solution)/shard_map/pallas_call | solution.py:558
Async XLA Ops:
  0.6 26.3 %copy-start.4 = (bf16[1024,256]{1,0:T(8,128)(2,1)S(1)}, bf16[1024,256]{1,0:T(8,128)(2,1)}, u32[]{:S(2)}) copy-start(bf16[1024,256]{1,0:T(8,128)(2,1)} %constant.9.clone.refs_2_) | copy-start | bytes 1572868
  0.6 26.3 %copy-start.5 = (bf16[1024,256]{1,0:T(8,128)(2,1)S(1)}, bf16[1024,256]{1,0:T(8,128)(2,1)}, u32[]{:S(2)}) copy-start(bf16[1024,256]{1,0:T(8,128)(2,1)} %constant.8.clone.refs_1_) | copy-start | bytes 1572868
  2.5 24.4 %copy-start.2 = (bf16[1024,256]{1,0:T(8,128)(2,1)S(1)}, bf16[1024,256]{1,0:T(8,128)(2,1)}, u32[]{:S(2)}) copy-start(bf16[1024,256]{1,0:T(8,128)(2,1)} %constant.11.clone.refs_4_) | copy-start | bytes 1572868
  2.5 24.4 %copy-start.3 = (bf16[1024,256]{1,0:T(8,128)(2,1)S(1)}, bf16[1024,256]{1,0:T(8,128)(2,1)}, u32[]{:S(2)}) copy-start(bf16[1024,256]{1,0:T(8,128)(2,1)} %constant.10.clone.refs_3_) | copy-start | bytes 1572868
  31.6 19.8 %copy-start = (bf16[1,128,1024]{2,1,0:T(8,128)(2,1)S(1)}, bf16[1,128,1024]{2,1,0:T(8,128)(2,1)}, u32[]{:S(2)}) copy-start(bf16[1,128,1024]{2,1,0:T(8,128)(2,1)} %gate_ref.1) | copy-start | bytes 786436
  31.6 19.8 %copy-start.1 = (bf16[1,128,1024]{2,1,0:T(8,128)(2,1)S(1)}, bf16[1,128,1024]{2,1,0:T(8,128)(2,1)}, u32[]{:S(2)}) copy-start(bf16[1,128,1024]{2,1,0:T(8,128)(2,1)} %upstream_ref.1) | copy-start | bytes 786436

commit v4 on v3

--- a/solution.py
+++ b/solution.py
@@ -293,15 +293,14 @@
     def rows_of(chunk):
         return slice(2 * CHUNK * chunk, 2 * CHUNK * (chunk + 1))
 
-    def forward(chunk):
+    def forward(chunk, start):
         rows = rows_of(chunk)
-        for start in (0, 2 * COLS, COLS):
-            columns = slice(start, start + COLS)
-            spectra_ref[rows, columns] = (
-                matmul(forward_high[rows, :], inputs_high[rows, columns])
-                + matmul(forward_low[rows, :], inputs_high[rows, columns])
-                + matmul(forward_high[rows, :], inputs_low[rows, columns])
-            )
+        columns = slice(start, start + COLS)
+        spectra_ref[rows, columns] = (
+            matmul(forward_high[rows, :], inputs_high[rows, columns])
+            + matmul(forward_low[rows, :], inputs_high[rows, columns])
+            + matmul(forward_high[rows, :], inputs_low[rows, columns])
+        )
 
     def backward(chunk):
         rows = rows_of(chunk)
@@ -315,10 +314,10 @@
             else:
                 classes_ref[rows, start : start + LANES] = made[:, :LANES] + made[:, LANES:]
 
-    forward(0)
+    for start in (2 * COLS, 0, COLS):
+        for chunk in range(chunks):
+            forward(chunk, start)
     for chunk in range(chunks):
-        if chunk + 1 < chunks:
-            forward(chunk + 1)
         for base in range(2 * CHUNK * chunk, 2 * CHUNK * chunk + CHUNK, STEP):
             spectra_step(spectra_ref, high_ref, low_ref, narrow, width, base)
         backward(chunk)

time: 53.3 us -> 53 us (level)
  no operation moved by 1% of the time
where the time goes in v4:
time: 53 us; the launch traced here: 52.8 us
  blocking collectives  44.1 us (83%)
  Pallas kernels  7.92 us (15%)
  between operations  0.71 us (1%)
    all_to_all x2, blocking collectives, exchange(): return lax.all_to_all(array, ('dp', 'seq'), 0, 0, tiled=True)  44.1 us
    pallas_call x1, Pallas kernels, packed_device(): call(kernel, [VM] * 5, shape_of(32 * CHUNK_ROWS, LANES), WORK, 24)  4.32 us
    pallas_call x1, Pallas kernels, packed_device(): call(pack_kernel, [HBM] * 6, shape_of(32, 72, 128), [stretch, pltpu.VMEM(...  1.87 us
    pallas_call x1, Pallas kernels, packed_device(): call(finish_kernel, [VM] * 3, (shape, shape, shape, shape_of(*filter_taps...  1.73 us

profile of v4, /device:TPU:0, one launch (start us, length us, event | category | flops | bytes accessed | tf_op | source)
XLA Modules:
  0.0 52.8 jit_solution(2613522502893897464)
XLA Ops:
  0.6 0.0 copy-start.4
  0.6 0.0 copy-start.5
  0.7 1.9 %shard_map.137 = bf16[32,72,128]{2,1,0:T(8,128)(2,1)S(1)} custom-call(bf16[1,128,1024]{2,1,0:T(8,128)(2,1)} %hidden_hbm.1, s32[1,128]{1,0:T(1,128)} %letters_hbm.1, bf16[1,128,1024]{2,1,0:T(8,128)(2,1)} %gate_ref.1, bf16[1,128,1024]{2,1,0:T(8,128)(2,1)} %upstream_ref.1, f32[4,1024]{1,0:T(4,128)} %embedding_hbm.1, bf16[4,8,1024]{2,1,0:T(8,128)(2,1)} %taps_hbm.1), custom_call_target="tpu_custom_call" | custom-call | tf_op jit(solution)/shard_map/pallas_call | solution.py:529
  2.5 0.0 copy-start.2
  2.5 0.0 copy-start.3
  2.6 24.4 %all_to_all.10.refs_0_ = bf16[32,72,128]{2,1,0:T(8,128)(2,1)S(1)} all-to-all(bf16[32,72,128]{2,1,0:T(8,128)(2,1)S(1)} %shard_map.137), channel_id=1, replica_groups=mesh['dp'=2,'seq'=16] {'dp','seq'}, dimensions={0} | all-to-all | bytes 1179648 | tf_op jit(solution)/shard_map/all_to_all | solution.py:524
  27.0 0.0 copy-done.4
  27.0 0.0 copy-done.5
  27.0 0.0 copy-done.2
  27.0 0.0 copy-done.3
  27.0 4.3 %shard_map.138 = bf16[2368,128]{1,0:T(8,128)(2,1)S(1)} custom-call(bf16[32,72,128]{2,1,0:T(8,128)(2,1)S(1)} %all_to_all.10.refs_0_, bf16[1024,256]{1,0:T(8,128)(2,1)S(1)} %copy-done.5, bf16[1024,256]{1,0:T(8,128)(2,1)S(1)} %copy-done.4, bf16[1024,256]{1,0:T(8,128)(2,1)S(1)} %copy-done.3, bf16[1024,256]{1,0:T(8,128)(2,1)S(1)} %copy-done.2), custom_call_target="tpu_custom_call" | custom-call | tf_op jit(solution)/shard_map/pallas_call | solution.py:548
  31.3 0.0 copy-start
  31.3 0.0 copy-start.1
  31.3 19.7 %all_to_all.11.receive_ref = bf16[32,37,2,128]{3,2,1,0:T(2,128)(2,1)S(1)} all-to-all(bf16[32,37,2,128]{3,2,1,0:T(2,128)(2,1)S(1)} %bitcast.1), channel_id=1, replica_groups=mesh['dp'=2,'seq'=16] {'dp','seq'}, dimensions={0} | all-to-all | bytes 1212416 | tf_op jit(solution)/shard_map/all_to_all | solution.py:524
  51.1 0.0 copy-done
  51.1 0.0 copy-done.1
  51.1 1.7 %shard_map.139 = (bf16[1,128,1024]{2,1,0:T(8,128)(2,1)}, bf16[1,128,1024]{2,1,0:T(8,128)(2,1)}, bf16[1,128,1024]{2,1,0:T(8,128)(2,1)}, f32[4,8,1024]{2,1,0:T(8,128)}, f32[4,1024]{1,0:T(4,128)}) custom-call(bf16[32,37,2,128]{3,2,1,0:T(2,128)(2,1)S(1)} %all_to_all.11.receive_ref, bf16[1,128,1024]{2,1,0:T(8,128)(2,1)S(1)} %copy-done, ...), custom_call_target="tpu_custom_call" | custom-call | tf_op jit(solution)/shard_map/pallas_call | solution.py:557
Async XLA Ops:
  0.6 26.3 %copy-start.4 = (bf16[1024,256]{1,0:T(8,128)(2,1)S(1)}, bf16[1024,256]{1,0:T(8,128)(2,1)}, u32[]{:S(2)}) copy-start(bf16[1024,256]{1,0:T(8,128)(2,1)} %constant.9.clone.refs_2_) | copy-start | bytes 1572868
  0.6 26.3 %copy-start.5 = (bf16[1024,256]{1,0:T(8,128)(2,1)S(1)}, bf16[1024,256]{1,0:T(8,128)(2,1)}, u32[]{:S(2)}) copy-start(bf16[1024,256]{1,0:T(8,128)(2,1)} %constant.8.clone.refs_1_) | copy-start | bytes 1572868
  2.5 24.4 %copy-start.2 = (bf16[1024,256]{1,0:T(8,128)(2,1)S(1)}, bf16[1024,256]{1,0:T(8,128)(2,1)}, u32[]{:S(2)}) copy-start(bf16[1024,256]{1,0:T(8,128)(2,1)} %constant.11.clone.refs_4_) | copy-start | bytes 1572868
  2.5 24.4 %copy-start.3 = (bf16[1024,256]{1,0:T(8,128)(2,1)S(1)}, bf16[1024,256]{1,0:T(8,128)(2,1)}, u32[]{:S(2)}) copy-start(bf16[1024,256]{1,0:T(8,128)(2,1)} %constant.10.clone.refs_3_) | copy-start | bytes 1572868
  31.3 19.8 %copy-start = (bf16[1,128,1024]{2,1,0:T(8,128)(2,1)S(1)}, bf16[1,128,1024]{2,1,0:T(8,128)(2,1)}, u32[]{:S(2)}) copy-start(bf16[1,128,1024]{2,1,0:T(8,128)(2,1)} %gate_ref.1) | copy-start | bytes 786436
  31.3 19.8 %copy-start.1 = (bf16[1,128,1024]{2,1,0:T(8,128)(2,1)S(1)}, bf16[1,128,1024]{2,1,0:T(8,128)(2,1)}, u32[]{:S(2)}) copy-start(bf16[1,128,1024]{2,1,0:T(8,128)(2,1)} %upstream_ref.1) | copy-start | bytes 786436

commit v5 on v4

--- a/solution.py
+++ b/solution.py
@@ -459,13 +459,6 @@
 
 def finish_kernel(receive_ref, gate_ref, upstream_ref, out_ref, hidden_ref, gated_ref, filter_ref, embedding_ref):
     back = return_channels()
-    for u, field in enumerate(received_columns(receive_ref, 0, back)):
-        for there, here in places_of(u):
-            out_ref[0, :, there] = (gate_ref[0, :, there].astype(F32) * field[:, here]).astype(BF16)
-            gated_ref[0, :, there] = (upstream_ref[0, :, there].astype(F32) * field[:, here]).astype(BF16)
-    for u, rows in enumerate(received_columns(receive_ref, 16, back)):
-        for there, here in places_of(u):
-            hidden_ref[0, :, there] = rows[:, here].astype(BF16)
     for u in range(4):
         columns = []
         for m in (2 * u, 2 * u + 1):
@@ -487,6 +480,13 @@
     for u in range(4):
         for there, here in places_of(u):
             embedding_ref[:, there] = done[4 * u : 4 * u + 4, here]
+    for u, field in enumerate(received_columns(receive_ref, 0, back)):
+        for there, here in places_of(u):
+            out_ref[0, :, there] = (gate_ref[0, :, there].astype(F32) * field[:, here]).astype(BF16)
+            gated_ref[0, :, there] = (upstream_ref[0, :, there].astype(F32) * field[:, here]).astype(BF16)
+    for u, rows in enumerate(received_columns(receive_ref, 16, back)):
+        for there, here in places_of(u):
+            hidden_ref[0, :, there] = rows[:, here].astype(BF16)
 
 
 WORK = [

time: 53 us -> 53 us (level)
  no operation moved by 1% of the time
where the time goes in v5:
time: 53 us; the launch traced here: 52.8 us
  blocking collectives  44.1 us (83%)
  Pallas kernels  7.91 us (15%)
  between operations  0.71 us (1%)
    all_to_all x2, blocking collectives, exchange(): return lax.all_to_all(array, ('dp', 'seq'), 0, 0, tiled=True)  44.1 us
    pallas_call x1, Pallas kernels, packed_device(): call(kernel, [VM] * 5, shape_of(32 * CHUNK_ROWS, LANES), WORK, 24)  4.32 us
    pallas_call x1, Pallas kernels, packed_device(): call(pack_kernel, [HBM] * 6, shape_of(32, 72, 128), [stretch, pltpu.VMEM(...  1.87 us
    pallas_call x1, Pallas kernels, packed_device(): call(finish_kernel, [VM] * 3, (shape, shape, shape, shape_of(*filter_taps...  1.72 us

profile of v5, /device:TPU:0, one launch (start us, length us, event | category | flops | bytes accessed | tf_op | source)
XLA Modules:
  0.0 52.8 jit_solution(17744464716397121919)
XLA Ops:
  0.6 0.0 copy-start.4
  0.6 0.0 copy-start.5
  0.7 1.9 %shard_map.137 = bf16[32,72,128]{2,1,0:T(8,128)(2,1)S(1)} custom-call(bf16[1,128,1024]{2,1,0:T(8,128)(2,1)} %hidden_hbm.1, s32[1,128]{1,0:T(1,128)} %letters_hbm.1, bf16[1,128,1024]{2,1,0:T(8,128)(2,1)} %gate_ref.1, bf16[1,128,1024]{2,1,0:T(8,128)(2,1)} %upstream_ref.1, f32[4,1024]{1,0:T(4,128)} %embedding_hbm.1, bf16[4,8,1024]{2,1,0:T(8,128)(2,1)} %taps_hbm.1), custom_call_target="tpu_custom_call" | custom-call | tf_op jit(solution)/shard_map/pallas_call | solution.py:529
  2.5 0.0 copy-start.2
  2.5 0.0 copy-start.3
  2.6 24.4 %all_to_all.10.refs_0_ = bf16[32,72,128]{2,1,0:T(8,128)(2,1)S(1)} all-to-all(bf16[32,72,128]{2,1,0:T(8,128)(2,1)S(1)} %shard_map.137), channel_id=1, replica_groups=mesh['dp'=2,'seq'=16] {'dp','seq'}, dimensions={0} | all-to-all | bytes 1179648 | tf_op jit(solution)/shard_map/all_to_all | solution.py:524
  27.0 0.0 copy-done.4
  27.0 0.0 copy-done.5
  27.0 0.0 copy-done.2
  27.0 0.0 copy-done.3
  27.0 4.3 %shard_map.138 = bf16[2368,128]{1,0:T(8,128)(2,1)S(1)} custom-call(bf16[32,72,128]{2,1,0:T(8,128)(2,1)S(1)} %all_to_all.10.refs_0_, bf16[1024,256]{1,0:T(8,128)(2,1)S(1)} %copy-done.5, bf16[1024,256]{1,0:T(8,128)(2,1)S(1)} %copy-done.4, bf16[1024,256]{1,0:T(8,128)(2,1)S(1)} %copy-done.3, bf16[1024,256]{1,0:T(8,128)(2,1)S(1)} %copy-done.2), custom_call_target="tpu_custom_call" | custom-call | tf_op jit(solution)/shard_map/pallas_call | solution.py:548
  31.3 0.0 copy-start
  31.3 0.0 copy-start.1
  31.3 19.7 %all_to_all.11.receive_ref = bf16[32,37,2,128]{3,2,1,0:T(2,128)(2,1)S(1)} all-to-all(bf16[32,37,2,128]{3,2,1,0:T(2,128)(2,1)S(1)} %bitcast.1), channel_id=1, replica_groups=mesh['dp'=2,'seq'=16] {'dp','seq'}, dimensions={0} | all-to-all | bytes 1212416 | tf_op jit(solution)/shard_map/all_to_all | solution.py:524
  51.1 0.0 copy-done
  51.1 0.0 copy-done.1
  51.1 1.7 %shard_map.139 = (bf16[1,128,1024]{2,1,0:T(8,128)(2,1)}, bf16[1,128,1024]{2,1,0:T(8,128)(2,1)}, bf16[1,128,1024]{2,1,0:T(8,128)(2,1)}, f32[4,8,1024]{2,1,0:T(8,128)}, f32[4,1024]{1,0:T(4,128)}) custom-call(bf16[32,37,2,128]{3,2,1,0:T(2,128)(2,1)S(1)} %all_to_all.11.receive_ref, bf16[1,128,1024]{2,1,0:T(8,128)(2,1)S(1)} %copy-done, ...), custom_call_target="tpu_custom_call" | custom-call | tf_op jit(solution)/shard_map/pallas_call | solution.py:557
Async XLA Ops:
  0.6 26.3 %copy-start.4 = (bf16[1024,256]{1,0:T(8,128)(2,1)S(1)}, bf16[1024,256]{1,0:T(8,128)(2,1)}, u32[]{:S(2)}) copy-start(bf16[1024,256]{1,0:T(8,128)(2,1)} %constant.9.clone.refs_2_) | copy-start | bytes 1572868
  0.6 26.3 %copy-start.5 = (bf16[1024,256]{1,0:T(8,128)(2,1)S(1)}, bf16[1024,256]{1,0:T(8,128)(2,1)}, u32[]{:S(2)}) copy-start(bf16[1024,256]{1,0:T(8,128)(2,1)} %constant.8.clone.refs_1_) | copy-start | bytes 1572868
  2.5 24.4 %copy-start.2 = (bf16[1024,256]{1,0:T(8,128)(2,1)S(1)}, bf16[1024,256]{1,0:T(8,128)(2,1)}, u32[]{:S(2)}) copy-start(bf16[1024,256]{1,0:T(8,128)(2,1)} %constant.11.clone.refs_4_) | copy-start | bytes 1572868
  2.5 24.4 %copy-start.3 = (bf16[1024,256]{1,0:T(8,128)(2,1)S(1)}, bf16[1024,256]{1,0:T(8,128)(2,1)}, u32[]{:S(2)}) copy-start(bf16[1024,256]{1,0:T(8,128)(2,1)} %constant.10.clone.refs_3_) | copy-start | bytes 1572868
  31.3 19.8 %copy-start = (bf16[1,128,1024]{2,1,0:T(8,128)(2,1)S(1)}, bf16[1,128,1024]{2,1,0:T(8,128)(2,1)}, u32[]{:S(2)}) copy-start(bf16[1,128,1024]{2,1,0:T(8,128)(2,1)} %gate_ref.1) | copy-start | bytes 786436
  31.3 19.8 %copy-start.1 = (bf16[1,128,1024]{2,1,0:T(8,128)(2,1)S(1)}, bf16[1,128,1024]{2,1,0:T(8,128)(2,1)}, u32[]{:S(2)}) copy-start(bf16[1,128,1024]{2,1,0:T(8,128)(2,1)} %upstream_ref.1) | copy-start | bytes 786436
